TPU v7x, 256 devices: a whole 4x4x8 slice. The times are simulated.
256 devices in a mesh: ctx: 4 (over x), head: 16 (over y, z_hi), seq: 4 (over z_lo, core).
Axes of the slice: x: 4, y: 4, z: 8 (z_hi: 4, z_lo: 2; z = z_hi * 2 + z_lo), core: 2. Of those that a mesh axis runs over, the one named last changes fastest.
Arguments:
- stretch_slot: int32 [32], P('seq'), parts along dimension 0, may hold values from 0 to 7, as said below
- gate_in: bfloat16 [2048, 8192], P(('seq', 'ctx'), 'head'), parts along dimension 0, may hold values from -6 to 6
- conv_in: bfloat16 [2048, 8192], P(('seq', 'ctx'), 'head'), parts along dimension 0, may hold values from -6 to 6
- value_in: bfloat16 [2048, 8192], P(('seq', 'ctx'), 'head'), parts along dimension 0, may hold values from -6 to 6
- modal_rate: float32 [64, 8192], P('seq', 'head'), parts along dimension 0, may hold values from 0.00048828125 to 0.05
- modal_residue: float32 [64, 8192], P('seq', 'head'), parts along dimension 0, may hold values from -0.078125 to 0.078125
- skip_gain: float32 [32768], P(('seq', 'head')), parts along dimension 0, may hold values from -4 to 4
- query_proj: bfloat16 [2048, 8192], P(('seq', 'ctx'), 'head'), parts along dimension 0, may hold values from -1024 to 1024
- key_proj: bfloat16 [2048, 8192], P(('seq', 'ctx'), 'head'), parts along dimension 0, may hold values from -256 to 256
- value_proj: bfloat16 [2048, 8192], P(('seq', 'ctx'), 'head'), parts along dimension 0, may hold values from -6 to 6
- out_weight: bfloat16 [32768, 8192], P(('seq', 'head')), parts along dimension 0, may hold values from -0.09375 to 0.09375
Outputs:
- mixed: bfloat16 [2048, 8192], P(('seq', 'ctx'), 'head'), parts along dimension 0
There are 4 independent parts, one for each index of `seq`. A program takes and returns all parts, laid end to end along the dimension named above; each array names one. Nothing has to cross between parts.
Inputs may be any that keep to these rules, and one draw needn't show every extreme that they name: Slot s holds stretch stretch_slot[s]; every stretch number appears exactly once.
All inputs are finite; a program needn't handle non-finite values.
Results may differ from a plain program's by a relative error of at most 0.015.
Values may be sent and summed in bfloat16 or wider, within the bound.
No kernel may reach another device: no remote copies, remote signals or barrier semaphores. Data moves between devices by JAX's collectives and lax.ppermute only.
A program may use at most 128 MiB of HBM per device.

v0:
```python
import math

import jax
import jax.numpy as jnp
from jax import lax
from jax.experimental import pallas as pl
from jax.experimental.pallas import tpu as pltpu
from jax.sharding import PartitionSpec as P


HD = 128
CH = 64
NY = 4
NZ = 4
F32 = jnp.float32
BF16 = jnp.bfloat16
NEG = -1e30

ORD_P = (0, 3, 1, 2)
ORD_Q = (0, 1, 3, 2)


def pack_kernel(
    conv_hbm, val_hbm, rate_hbm, key_hbm, value_hbm, res_hbm, skip_hbm,
    a_ref, b_ref, p_ref, rate_ref, res_ref, skip_ref, conv_scr, val_scr, sems,
):
    rows, channels = conv_scr.shape
    modes = rate_ref.shape[0]
    sources = (conv_hbm, val_hbm, rate_hbm, key_hbm, value_hbm, res_hbm, skip_hbm)
    targets = (
        conv_scr, val_scr, rate_ref, a_ref.at[pl.ds(0, rows), :], b_ref.at[pl.ds(0, rows), :], res_ref, skip_ref
    )
    copies = [pltpu.make_async_copy(s, t, sems.at[i]) for i, (s, t) in enumerate(zip(sources, targets))]
    for copy in copies:
        copy.start()
    for copy in copies[:3]:
        copy.wait()
    p_ref[...] = conv_scr[...].astype(F32) * val_scr[...].astype(F32)
    decay = jnp.exp(-rate_ref[...])
    states = [jnp.zeros((modes, channels), F32) for _ in range(2)]
    for j in range(CH):
        for m in range(2):
            states[m] = decay * states[m] + p_ref[m * CH + j : m * CH + j + 1, :]
    a_ref[rows:, :] = states[0].astype(BF16)
    b_ref[rows:, :] = states[1].astype(BF16)
    for copy in copies[3:]:
        copy.wait()


def pack_stage(conv_in, value_in, rate, keys, values, residue, skip):
    rows, channels = conv_in.shape
    modes = rate.shape[0]
    vmem = pl.BlockSpec(memory_space=pltpu.VMEM)
    hbm = pl.BlockSpec(memory_space=pltpu.HBM)
    return pl.pallas_call(
        pack_kernel,
        in_specs=[hbm] * 7,
        out_specs=[vmem] * 6,
        out_shape=[
            jax.ShapeDtypeStruct((rows + modes, channels), BF16),
            jax.ShapeDtypeStruct((rows + modes, channels), BF16),
            jax.ShapeDtypeStruct((rows, channels), F32),
            jax.ShapeDtypeStruct(rate.shape, F32),
            jax.ShapeDtypeStruct(residue.shape, F32),
            jax.ShapeDtypeStruct(skip.shape, F32),
        ],
        scratch_shapes=[
            pltpu.VMEM((rows, channels), BF16),
            pltpu.VMEM((rows, channels), BF16),
            pltpu.SemaphoreType.DMA((7,)),
        ],
        compiler_params=pltpu.CompilerParams(vmem_limit_bytes=4 << 20),
        name="pack_states",
    )(conv_in, value_in, rate, keys, values, residue, skip)


BLOCKS = 4


def weight_loads(weight_hbm, weight_ref, sems, start):
    block = weight_ref.shape[0] // BLOCKS
    loads = [
        pltpu.make_async_copy(
            weight_hbm.at[pl.ds(start + i * block, block), :], weight_ref.at[pl.ds(i * block, block), :], sems.at[i]
        )
        for i in range(BLOCKS)
    ]
    for load in loads:
        load.start()
    return loads


CHUNKS = [(a, b) for a in (2, 1, 3, 0) for b in (2, 1, 3, 0)]


def local_kernel(p_ref, rate_ref, res_ref, skip_ref, weight_hbm, base_ref, weight_ref, h_scr, wsems):
    channels = p_ref.shape[1]
    modes = rate_ref.shape[0]
    heads = channels // HD
    loads = weight_loads(weight_hbm, weight_ref, wsems, 0)
    index = lax.broadcasted_iota(jnp.int32, (8, HD), 0)
    index_f = index.astype(F32)

    for h in range(heads):
        at = slice(h * HD, (h + 1) * HD)
        step8 = jnp.exp(-8.0 * rate_ref[:, at])
        taps = [jnp.zeros((8, HD), F32) for _ in range(8)]
        for n in range(modes):
            term = res_ref[n : n + 1, at] * jnp.exp(-rate_ref[n : n + 1, at] * index_f)
            factor = jnp.broadcast_to(step8[n : n + 1, :], (8, HD))
            for k in range(8):
                taps[k] = taps[k] + term
                if k < 7:
                    term = term * factor
        for s in range(8):
            previous = jnp.zeros((8, HD), F32)
            for k in range(8):
                if s == 0:
                    shifted = taps[k]
                else:
                    rolled = pltpu.roll(taps[k], s, 0)
                    shifted = jnp.where(index < s, previous, rolled)
                    previous = rolled
                h_scr[s * 64 + 8 * k : s * 64 + 8 * k + 8, :] = shifted
        skip = skip_ref[:, at]
        acc = [[jnp.zeros((8, HD), F32) for _ in range(8)] for _ in range(2)]
        for j in range(CH):
            jt, s = j // 8, j % 8
            wide = [jnp.broadcast_to(p_ref[m * CH + j : m * CH + j + 1, at], (8, HD)) for m in range(2)]
            for it in range(jt, 8):
                tap = h_scr[s * 64 + 8 * (it - jt) : s * 64 + 8 * (it - jt) + 8, :]
                for m in range(2):
                    acc[m][it] = acc[m][it] + tap * wide[m]
        for m in range(2):
            for it in range(8):
                row = m * CH + 8 * it
                base_ref[row : row + 8, at] = acc[m][it] + skip * p_ref[row : row + 8, at]
    for load in loads:
        load.wait()


def local_stage(product, rate, residue, skip, weight):
    vmem = pl.BlockSpec(memory_space=pltpu.VMEM)
    return pl.pallas_call(
        local_kernel,
        in_specs=[vmem] * 4 + [pl.BlockSpec(memory_space=pltpu.HBM)],
        out_specs=[vmem] * 2,
        out_shape=[
            jax.ShapeDtypeStruct(product.shape, F32),
            jax.ShapeDtypeStruct((weight.shape[0] // 2, weight.shape[1]), BF16),
        ],
        scratch_shapes=[pltpu.VMEM((512, HD), F32), pltpu.SemaphoreType.DMA((BLOCKS,))],
        compiler_params=pltpu.CompilerParams(vmem_limit_bytes=8 << 20),
        name="local_conv",
    )(product, rate, residue, skip, weight)


def fetch_kernel(
    rate_ref, res_ref, slot_hbm, query_hbm, gate_hbm, weight_hbm,
    bias_ref, pull_ref, query_ref, gate_ref, weight_ref, slot_ref, sems, wsems,
):
    rows = query_ref.shape[0]
    ctx = lax.axis_index("ctx")
    sources = (slot_hbm, query_hbm, gate_hbm)
    targets = (slot_ref, query_ref, gate_ref)
    copies = [pltpu.make_async_copy(s, t, sems.at[i]) for i, (s, t) in enumerate(zip(sources, targets))]
    for copy in copies:
        copy.start()
    loads = weight_loads(weight_hbm, weight_ref, wsems, weight_ref.shape[0])
    for copy in copies:
        copy.wait()
    key_st = [slot_ref[2 * (ctx ^ m) + s] for m in (0, 1, 3, 2) for s in range(2)]
    my_st = key_st[:2]
    col = lax.broadcasted_iota(jnp.int32, (rows, HD), 1)
    row = lax.broadcasted_iota(jnp.int32, (rows, HD), 0)
    q_pos = jnp.where(row < CH, my_st[0] * CH + row, my_st[1] * CH + row - CH)
    for r in range(4):
        k_pos = jnp.where(col < CH, key_st[2 * r] * CH + col, key_st[2 * r + 1] * CH + col - CH)
        bias_ref[r] = jnp.where(k_pos <= q_pos, 0.0, NEG)
    for m in range(2):
        for i, stretch in enumerate(key_st):
            gap = my_st[m] - 1 - stretch
            span = (CH * jnp.maximum(gap, 0)).astype(F32)
            pull_ref[m, i] = jnp.where(gap >= 0, 1.0, 0.0) * (res_ref[...] * jnp.exp(-rate_ref[...] * span))
    for load in loads:
        load.wait()


def fetch_stage(rate, residue, slots, query, gate, weight):
    rows, channels = query.shape
    vmem = pl.BlockSpec(memory_space=pltpu.VMEM)
    hbm = pl.BlockSpec(memory_space=pltpu.HBM)
    return pl.pallas_call(
        fetch_kernel,
        in_specs=[vmem] * 2 + [hbm] * 4,
        out_specs=[vmem] * 5,
        out_shape=[
            jax.ShapeDtypeStruct((4, rows, HD), F32),
            jax.ShapeDtypeStruct((2, 8) + rate.shape, F32),
            jax.ShapeDtypeStruct(query.shape, BF16),
            jax.ShapeDtypeStruct(gate.shape, BF16),
            jax.ShapeDtypeStruct((weight.shape[0] // 2, channels * NY * NZ), BF16),
        ],
        scratch_shapes=[
            pltpu.SMEM(slots.shape, jnp.int32),
            pltpu.SemaphoreType.DMA((3,)),
            pltpu.SemaphoreType.DMA((BLOCKS,)),
        ],
        compiler_params=pltpu.CompilerParams(vmem_limit_bytes=8 << 20),
        name="fetch_weight",
    )(rate, residue, slots, query, gate, weight)


def mix_kernel(
    a0, a1, a3, a2, b0, b1, b3, b2, base_ref, bias_ref, pull_ref, rate_ref, query_ref, gate_ref, w0, w1,
    send_p, send_q, keep_p, keep_q, comb_scr,
):
    rows, channels = query_ref.shape
    modes = rate_ref.shape[0]
    heads = channels // HD
    first = (a0, a1, a3, a2)
    second = (b0, b1, b3, b2)
    rows_f = (lax.broadcasted_iota(jnp.int32, (8, HD), 0) + 1).astype(F32)
    scale = 1.0 / math.sqrt(HD)
    for h in range(heads):
        at = slice(h * HD, (h + 1) * HD)
        rate = rate_ref[:, at]
        pieces = [s[rows:, at].astype(F32) for pair in zip(first, second) for s in pair]
        entry = []
        for m in range(2):
            total = pull_ref[m, 0, :, at] * pieces[0]
            for i in range(1, 8):
                total = total + pull_ref[m, i, :, at] * pieces[i]
            entry.append(total)
        step8 = jnp.exp(-8.0 * rate)
        carry = [[jnp.zeros((8, HD), F32) for _ in range(8)] for _ in range(2)]
        for n in range(modes):
            term = jnp.exp(-rate[n : n + 1, :] * rows_f)
            factor = jnp.broadcast_to(step8[n : n + 1, :], (8, HD))
            wide = [jnp.broadcast_to(entry[m][n : n + 1, :], (8, HD)) for m in range(2)]
            for k in range(8):
                for m in range(2):
                    carry[m][k] = carry[m][k] + term * wide[m]
                if k < 7:
                    term = term * factor
        carried = jnp.concatenate([carry[m][k] for m in range(2) for k in range(8)], axis=0)
        hyena = gate_ref[:, at].astype(F32) * (base_ref[:, at] + carried)
        query = query_ref[:, at]
        scores = [
            lax.dot_general(query, k[:rows, at], (((1,), (1,)), ((), ())), preferred_element_type=F32) * scale
            + bias_ref[r]
            for r, k in enumerate(first)
        ]
        peak = jnp.maximum(jnp.maximum(scores[0], scores[1]), jnp.maximum(scores[2], scores[3]))
        peak = jnp.max(peak, axis=1, keepdims=True)
        probs = [jnp.exp(s - peak) for s in scores]
        total = jnp.sum((probs[0] + probs[1]) + (probs[2] + probs[3]), axis=1, keepdims=True)
        mixed = None
        for p, v in zip(probs, second):
            part = jnp.dot(p.astype(BF16), v[:rows, at], preferred_element_type=F32)
            mixed = part if mixed is None else mixed + part
        comb_scr[:, at] = (hyena + mixed / total).astype(BF16)
    comb = comb_scr[...]
    head = lax.axis_index("head")
    my_y, my_z = head // NZ, head % NZ
    for a, b in CHUNKS:
        chunk = (my_y ^ a) * NZ + (my_z ^ b)
        at = pl.ds(pl.multiple_of(chunk * channels, channels), channels)
        half = channels // 2
        part = jnp.dot(comb[:, :half], w0[:, at], preferred_element_type=F32)
        part = part + jnp.dot(comb[:, half:], w1[:, at], preferred_element_type=F32)
        for which, (send, keep) in enumerate(((send_p, keep_p), (send_q, keep_q))):
            orders = ORD_P if which == 0 else ORD_Q
            x = orders.index(a)
            y = orders.index(b)
            block = part[CH * which : CH * which + CH, :].astype(BF16)
            if x < 2:
                keep[x, y] = block
            else:
                send[x - 2, y] = block


def mix_stage(first, second, base, bias, pull, rate, query, gate, w0, w1):
    rows, channels = query.shape
    vmem = pl.BlockSpec(memory_space=pltpu.VMEM)
    return pl.pallas_call(
        mix_kernel,
        in_specs=[vmem] * 16,
        out_specs=[vmem] * 4,
        out_shape=[jax.ShapeDtypeStruct((2, 4, CH, channels), BF16)] * 4,
        scratch_shapes=[pltpu.VMEM((rows, channels), BF16)],
        compiler_params=pltpu.CompilerParams(vmem_limit_bytes=20 << 20),
        name="mix_project",
    )(*first, *second, base, bias, pull, rate, query, gate, w0, w1)


def swap(value, axis, mask):
    if axis == "ctx":
        pairs = [(i, i ^ mask) for i in range(4)]
        return lax.ppermute(value, "ctx", pairs)
    if axis == "y":
        pairs = [(y * NZ + z, (y ^ mask) * NZ + z) for y in range(NY) for z in range(NZ)]
    else:
        pairs = [(y * NZ + z, y * NZ + (z ^ mask)) for y in range(NY) for z in range(NZ)]
    return lax.ppermute(value, "head", pairs)


def body(
    stretch_slot, gate_in, conv_in, value_in, modal_rate, modal_residue, skip_gain, query_proj, key_proj, value_proj,
    out_weight,
):
    conv_in, value_in, key_proj, value_proj, query_proj, gate_in, out_weight, modal_rate, modal_residue = (
        pltpu.with_memory_space_constraint(x, pltpu.HBM)
        for x in (
            conv_in, value_in, key_proj, value_proj, query_proj, gate_in, out_weight, modal_rate, modal_residue
        )
    )
    slots = pltpu.with_memory_space_constraint(stretch_slot, pltpu.HBM)
    skip = pltpu.with_memory_space_constraint(skip_gain[None, :], pltpu.HBM)
    own_a, own_b, product, rate, residue, skip = pack_stage(
        conv_in, value_in, modal_rate, key_proj, value_proj, modal_residue, skip
    )

    def gather(value, mask):
        return swap(value, "ctx", mask)

    one_a = gather(own_a, 1)
    three_b = gather(own_b, 3)
    one_b = gather(own_b, 1)
    three_a = gather(own_a, 3)
    two_a = gather(one_a, 3)
    two_b = gather(three_b, 1)
    base, w0 = local_stage(product, rate, residue, skip, out_weight)
    bias, pull, query, gate, w1 = fetch_stage(rate, residue, slots, query_proj, gate_in, out_weight)
    send_p, send_q, keep_p, keep_q = mix_stage(
        (own_a, one_a, three_a, two_a), (own_b, one_b, three_b, two_b), base, bias, pull, rate, query, gate, w0, w1
    )

    def total(*terms):
        result = terms[0].astype(F32)
        for term in terms[1:]:
            result = result + term.astype(F32)
        return result.astype(BF16)

    keeps = (keep_p, keep_q)
    plans = ((("y", 1), ("y", 3), ("z", 1), ("z", 3)), (("y", 3), ("y", 1), ("z", 3), ("z", 1)))
    first = [swap(send, *plan[0]) for send, plan in zip((send_p, send_q), plans)]
    second = [swap(total(k[1], a[1]), *plan[1]) for k, a, plan in zip(keeps, first, plans)]
    third = [swap(total(k[0, 2:], a[0, 2:], b[2:]), *plan[2]) for k, a, b, plan in zip(keeps, first, second, plans)]
    fourth = [
        swap(total(k[0, 1], a[0, 1], b[1], c[1]), *plan[3])
        for k, a, b, c, plan in zip(keeps, first, second, third, plans)
    ]
    parts = [
        total(k[0, 0], a[0, 0], b[0], c[0], d) for k, a, b, c, d in zip(keeps, first, second, third, fourth)
    ]
    return jnp.concatenate(parts, axis=0)


def solution(mesh):
    return jax.shard_map(
        body,
        mesh=mesh,
        in_specs=(
            P("seq"),
            P(("seq", "ctx"), "head"),
            P(("seq", "ctx"), "head"),
            P(("seq", "ctx"), "head"),
            P("seq", "head"),
            P("seq", "head"),
            P(("seq", "head")),
            P(("seq", "ctx"), "head"),
            P(("seq", "ctx"), "head"),
            P(("seq", "ctx"), "head"),
            P(("seq", "head"), None),
        ),
        out_specs=P(("seq", "ctx"), "head"),
        check_vma=False,
    )
```

profile of v0, /device:TPU:2, one launch (start us, length us, event | category | flops | bytes accessed | tf_op | source)
XLA Modules:
  0.0 58.4 jit_solution(10201275037460035036)
XLA Ops:
  0.0 1.4 %pack_states.1 = (bf16[144,512]{1,0:T(8,128)(2,1)S(1)}, bf16[144,512]{1,0:T(8,128)(2,1)S(1)}, f32[128,512]{1,0:T(8,128)S(1)}, f32[16,512]{1,0:T(8,128)S(1)}, f32...) custom-call(bf16[128,512]{1,0:T(8,128)(2,1)} %conv_hbm.1, bf16[128,512]{1,0:T(8,128)(2,1)} %val_hbm.1, f32[16,512]{1,0:T(8,128)} %rate_hbm.1, ...), custom_call_target="tpu_custom_call" | custom-call | tf_op jit(solution)/shard_map/pack_states/pallas_call | solution.py:55
  1.4 2.3 %collective-permute-start = (bf16[144,512]{1,0:T(8,128)(2,1)S(1)}, bf16[144,512]{1,0:T(8,128)(2,1)S(1)}, u32[]{:S(2)}, u32[]{:S(2)}) collective-permute-start(bf16[144,512]{1,0:T(8,128)(2,1)S(1)} %get-tuple-element.22.a0), channel_id=1, source_target_pairs={{0,64},{64,0},{128,192},{192,128},{1,65},{65,1},{129,193},{193,129... | collective-permute-start | bytes 442376 | tf_op jit(solution)/shard_map/ppermute | solution.py:300
  3.7 0.4 collective-permute-start.4
  4.1 1.6 %collective-permute-start.1 = (bf16[144,512]{1,0:T(8,128)(2,1)S(1)}, bf16[144,512]{1,0:T(8,128)(2,1)S(1)}, u32[]{:S(2)}, u32[]{:S(2)}) collective-permute-start(bf16[144,512]{1,0:T(8,128)(2,1)S(1)} %get-tuple-element.22.a0), channel_id=1, source_target_pairs={{0,192},{64,128},{128,64},{192,0},{1,193},{65,129},{129,65},{193,1... | collective-permute-start | bytes 442376 | tf_op jit(solution)/shard_map/ppermute | solution.py:300
  5.7 1.3 %collective-permute-start.3 = (bf16[144,512]{1,0:T(8,128)(2,1)S(1)}, bf16[144,512]{1,0:T(8,128)(2,1)S(1)}, u32[]{:S(2)}, u32[]{:S(2)}) collective-permute-start(bf16[144,512]{1,0:T(8,128)(2,1)S(1)} %get-tuple-element.23.b0), channel_id=1, source_target_pairs={{0,64},{64,0},{128,192},{192,128},{1,65},{65,1},{129,193},{193,129... | collective-permute-start | bytes 442376 | tf_op jit(solution)/shard_map/ppermute | solution.py:300
  7.0 0.5 collective-permute-done.a1
  7.5 1.5 %collective-permute-start.2 = (bf16[144,512]{1,0:T(8,128)(2,1)S(1)}, bf16[144,512]{1,0:T(8,128)(2,1)S(1)}, u32[]{:S(2)}, u32[]{:S(2)}) collective-permute-start(bf16[144,512]{1,0:T(8,128)(2,1)S(1)} %collective-permute-done.a1), channel_id=1, source_target_pairs={{0,192},{64,128},{128,64},{192,0},{1,193},{65,129},{129,65},{193,1... | collective-permute-start | bytes 442376 | tf_op jit(solution)/shard_map/ppermute | solution.py:300
  9.0 1.2 %collective-permute-done.4.b3 = bf16[144,512]{1,0:T(8,128)(2,1)S(1)} collective-permute-done((bf16[144,512]{1,0:T(8,128)(2,1)S(1)}, bf16[144,512]{1,0:T(8,128)(2,1)S(1)}, u32[]{:S(2)}, u32[]{:S(2)}) %collective-permute-start.4) | collective-permute-done | bytes 147488 | tf_op jit(solution)/shard_map/ppermute | solution.py:300
  10.2 1.5 %collective-permute-start.5 = (bf16[144,512]{1,0:T(8,128)(2,1)S(1)}, bf16[144,512]{1,0:T(8,128)(2,1)S(1)}, u32[]{:S(2)}, u32[]{:S(2)}) collective-permute-start(bf16[144,512]{1,0:T(8,128)(2,1)S(1)} %collective-permute-done.4.b3), channel_id=1, source_target_pairs={{0,64},{64,0},{128,192},{192,128},{1,65},{65,1},{129,193},{193,129... | collective-permute-start | bytes 442376 | tf_op jit(solution)/shard_map/ppermute | solution.py:300
  11.6 2.2 %local_conv.1 = (f32[128,512]{1,0:T(8,128)S(1)}, bf16[256,8192]{1,0:T(8,128)(2,1)S(1)}) custom-call(f32[128,512]{1,0:T(8,128)S(1)} %get-tuple-element.24.p_ref, f32[16,512]{1,0:T(8,128)S(1)} %get-tuple-element.25.rate_ref, f32[16,512]{1,0:T(8,128)S(1)} %get-tuple-element.26.res_ref, f32[1,512]{1,0:T(1,128)S(1)} %get-tuple-element.27.skip_ref, ...), custom_call_target="tpu_custom_call" | custom-call | tf_op jit(solution)/shard_map/local_conv/pallas_call | solution.py:144
  13.9 2.3 %fetch_weight.1 = (f32[4,128,128]{2,1,0:T(8,128)S(1)}, f32[2,8,16,512]{3,2,1,0:T(8,128)S(1)}, bf16[128,512]{1,0:T(8,128)(2,1)S(1)}, bf16[128,512]{1,0:T(8,128)(2,1)S(1)}, bf16[256,8192]{1,0:T(8,128)(2,1)S(1)}) custom-call(f32[16,512]{1,0:T(8,128)S(1)} %get-tuple-element.25.rate_ref, f32[16,512]{1,0:T(8,128)S(1)} %get-tuple-element.26.res_ref, s32[8]{0:T(128)} %slot_hbm.1, ...), custom_call_target="tpu_custom_call" | custom-call | tf_op jit(solution)/shard_map/fetch_weight/pallas_call | solution.py:193
  16.2 3.1 %mix_project.1 = (bf16[2,4,64,512]{3,2,1,0:T(8,128)(2,1)S(1)}, bf16[2,4,64,512]{3,2,1,0:T(8,128)(2,1)S(1)}, bf16[2,4,64,512]{3,2,1,0:T(8,128)(2,1)S(1)}, bf16[2,4,64,512]{3,2,1,0:T(8,128)(2,1)S(1)}) custom-call(bf16[144,512]{1,0:T(8,128)(2,1)S(1)} %get-tuple-element.22.a0, bf16[144,512]{1,0:T(8,128)(2,1)S(1)} %collective-permute-done.a1, ...), custom_call_target="tpu_custom_call" | custom-call | tf_op jit(solution)/shard_map/mix_project/pallas_call | solution.py:286
  19.3 1.4 %collective-permute-start.6 = (bf16[2,4,64,512]{3,2,1,0:T(8,128)(2,1)S(1)}, bf16[2,4,64,512]{3,2,1,0:T(8,128)(2,1)S(1)}, u32[]{:S(2)}, u32[]{:S(2)}) collective-permute-start(bf16[2,4,64,512]{3,2,1,0:T(8,128)(2,1)S(1)} %get-tuple-element.36), channel_id=1, source_target_pairs={{0,16},{4,20},{8,24},{12,28},{16,0},{20,4},{24,8},{28,12},{32,48},... | collective-permute-start | bytes 1572872 | tf_op jit(solution)/shard_map/ppermute | solution.py:305
  20.6 2.2 %collective-permute-start.10 = (bf16[2,4,64,512]{3,2,1,0:T(8,128)(2,1)S(1)}, bf16[2,4,64,512]{3,2,1,0:T(8,128)(2,1)S(1)}, u32[]{:S(2)}, u32[]{:S(2)}) collective-permute-start(bf16[2,4,64,512]{3,2,1,0:T(8,128)(2,1)S(1)} %get-tuple-element.38), channel_id=1, source_target_pairs={{0,48},{4,52},{8,56},{12,60},{16,32},{20,36},{24,40},{28,44},{32,1... | collective-permute-start | bytes 1572872 | tf_op jit(solution)/shard_map/ppermute | solution.py:305
  22.8 7.5 %collective-permute-done.6 = bf16[2,4,64,512]{3,2,1,0:T(8,128)(2,1)S(1)} collective-permute-done((bf16[2,4,64,512]{3,2,1,0:T(8,128)(2,1)S(1)}, bf16[2,4,64,512]{3,2,1,0:T(8,128)(2,1)S(1)}, u32[]{:S(2)}, u32[]{:S(2)}) %collective-permute-start.6) | collective-permute-done | bytes 524320 | tf_op jit(solution)/shard_map/ppermute | solution.py:305
  30.4 3.1 %collective-permute-start.7 = (bf16[4,64,512]{2,1,0:T(8,128)(2,1)S(1)}, bf16[4,64,512]{2,1,0:T(8,128)(2,1)S(1)}, u32[]{:S(2)}, u32[]{:S(2)}) collective-permute-start(bf16[4,64,512]{2,1,0:T(8,128)(2,1)S(1)} %fusion), channel_id=1, source_target_pairs={{0,48},{4,52},{8,56},{12,60},{16,32},{20,36},{24,40},{28,44},{32,1... | collective-permute-start | bytes 786440 | tf_op jit(solution)/shard_map/ppermute | solution.py:305
  33.5 1.3 %collective-permute-done.10 = bf16[2,4,64,512]{3,2,1,0:T(8,128)(2,1)S(1)} collective-permute-done((bf16[2,4,64,512]{3,2,1,0:T(8,128)(2,1)S(1)}, bf16[2,4,64,512]{3,2,1,0:T(8,128)(2,1)S(1)}, u32[]{:S(2)}, u32[]{:S(2)}) %collective-permute-start.10) | collective-permute-done | bytes 524320 | tf_op jit(solution)/shard_map/ppermute | solution.py:305
  34.9 3.5 %collective-permute-done.7 = bf16[4,64,512]{2,1,0:T(8,128)(2,1)S(1)} collective-permute-done((bf16[4,64,512]{2,1,0:T(8,128)(2,1)S(1)}, bf16[4,64,512]{2,1,0:T(8,128)(2,1)S(1)}, u32[]{:S(2)}, u32[]{:S(2)}) %collective-permute-start.7) | collective-permute-done | bytes 262176 | tf_op jit(solution)/shard_map/ppermute | solution.py:305
  38.5 3.4 %collective-permute-start.8 = (bf16[2,64,512]{2,1,0:T(8,128)(2,1)S(1)}, bf16[2,64,512]{2,1,0:T(8,128)(2,1)S(1)}, u32[]{:S(2)}, u32[]{:S(2)}) collective-permute-start(bf16[2,64,512]{2,1,0:T(8,128)(2,1)S(1)} %fusion.3), channel_id=1, source_target_pairs={{0,4},{4,0},{8,12},{12,8},{16,20},{20,16},{24,28},{28,24},{32,36},... | collective-permute-start | bytes 393224 | tf_op jit(solution)/shard_map/ppermute | solution.py:305
  41.9 5.8 %collective-permute-start.12 = (bf16[2,64,512]{2,1,0:T(8,128)(2,1)S(1)}, bf16[2,64,512]{2,1,0:T(8,128)(2,1)S(1)}, u32[]{:S(2)}, u32[]{:S(2)}) collective-permute-start(bf16[2,64,512]{2,1,0:T(8,128)(2,1)S(1)} %fusion.2), channel_id=1, source_target_pairs={{0,12},{4,8},{8,4},{12,0},{16,28},{20,24},{24,20},{28,16},{32,44},... | collective-permute-start | bytes 393224 | tf_op jit(solution)/shard_map/ppermute | solution.py:305
  47.8 4.3 %collective-permute-start.9 = (bf16[64,512]{1,0:T(8,128)(2,1)S(1)}, bf16[64,512]{1,0:T(8,128)(2,1)S(1)}, u32[]{:S(2)}, u32[]{:S(2)}) collective-permute-start(bf16[64,512]{1,0:T(8,128)(2,1)S(1)} %fusion.7), channel_id=1, source_target_pairs={{0,12},{4,8},{8,4},{12,0},{16,28},{20,24},{24,20},{28,16},{32,44},... | collective-permute-start | bytes 196616 | tf_op jit(solution)/shard_map/ppermute | solution.py:305
  52.4 2.7 %collective-permute-start.13 = (bf16[64,512]{1,0:T(8,128)(2,1)S(1)}, bf16[64,512]{1,0:T(8,128)(2,1)S(1)}, u32[]{:S(2)}, u32[]{:S(2)}) collective-permute-start(bf16[64,512]{1,0:T(8,128)(2,1)S(1)} %fusion.4), channel_id=1, source_target_pairs={{0,4},{4,0},{8,12},{12,8},{16,20},{20,16},{24,28},{28,24},{32,36},... | collective-permute-start | bytes 196616 | tf_op jit(solution)/shard_map/ppermute | solution.py:305
  55.1 2.5 %collective-permute-done.13 = bf16[64,512]{1,0:T(8,128)(2,1)S(1)} collective-permute-done((bf16[64,512]{1,0:T(8,128)(2,1)S(1)}, bf16[64,512]{1,0:T(8,128)(2,1)S(1)}, u32[]{:S(2)}, u32[]{:S(2)}) %collective-permute-start.13) | collective-permute-done | bytes 65568 | tf_op jit(solution)/shard_map/ppermute | solution.py:305
  57.7 0.7 %pad_maximum_fusion = bf16[128,512]{1,0:T(8,128)(2,1)} fusion(bf16[64,512]{1,0:T(8,128)(2,1)S(1)} %fusion.6, bf16[64,512]{1,0:T(8,128)(2,1)S(1)} %fusion.9), kind=kLoop, calls=%fused_computation.8 | loop fusion | flops 262144 | bytes 262144 | tf_op jit(solution)/shard_map/concatenate | solution.py:357
  (17 shorter events, 0.8 us)
Async XLA Ops:
  1.4 6.2 %collective-permute-start = (bf16[144,512]{1,0:T(8,128)(2,1)S(1)}, bf16[144,512]{1,0:T(8,128)(2,1)S(1)}, u32[]{:S(2)}, u32[]{:S(2)}) collective-permute-start(bf16[144,512]{1,0:T(8,128)(2,1)S(1)} %get-tuple-element.22.a0), channel_id=1, source_target_pairs={{0,64},{64,0},{128,192},{192,128},{1,65},{65,1},{129,193},{193,129... | collective-permute-start | bytes 442376 | tf_op jit(solution)/shard_map/ppermute | solution.py:300
  3.7 6.5 %collective-permute-start.4 = (bf16[144,512]{1,0:T(8,128)(2,1)S(1)}, bf16[144,512]{1,0:T(8,128)(2,1)S(1)}, u32[]{:S(2)}, u32[]{:S(2)}) collective-permute-start(bf16[144,512]{1,0:T(8,128)(2,1)S(1)} %get-tuple-element.23.b0), channel_id=1, source_target_pairs={{0,192},{64,128},{128,64},{192,0},{1,193},{65,129},{129,65},{193,1... | collective-permute-start | bytes 442376 | tf_op jit(solution)/shard_map/ppermute | solution.py:300
  4.1 12.0 %collective-permute-start.1 = (bf16[144,512]{1,0:T(8,128)(2,1)S(1)}, bf16[144,512]{1,0:T(8,128)(2,1)S(1)}, u32[]{:S(2)}, u32[]{:S(2)}) collective-permute-start(bf16[144,512]{1,0:T(8,128)(2,1)S(1)} %get-tuple-element.22.a0), channel_id=1, source_target_pairs={{0,192},{64,128},{128,64},{192,0},{1,193},{65,129},{129,65},{193,1... | collective-permute-start | bytes 442376 | tf_op jit(solution)/shard_map/ppermute | solution.py:300
  5.7 10.5 %collective-permute-start.3 = (bf16[144,512]{1,0:T(8,128)(2,1)S(1)}, bf16[144,512]{1,0:T(8,128)(2,1)S(1)}, u32[]{:S(2)}, u32[]{:S(2)}) collective-permute-start(bf16[144,512]{1,0:T(8,128)(2,1)S(1)} %get-tuple-element.23.b0), channel_id=1, source_target_pairs={{0,64},{64,0},{128,192},{192,128},{1,65},{65,1},{129,193},{193,129... | collective-permute-start | bytes 442376 | tf_op jit(solution)/shard_map/ppermute | solution.py:300
  7.5 8.7 %collective-permute-start.2 = (bf16[144,512]{1,0:T(8,128)(2,1)S(1)}, bf16[144,512]{1,0:T(8,128)(2,1)S(1)}, u32[]{:S(2)}, u32[]{:S(2)}) collective-permute-start(bf16[144,512]{1,0:T(8,128)(2,1)S(1)} %collective-permute-done.a1), channel_id=1, source_target_pairs={{0,192},{64,128},{128,64},{192,0},{1,193},{65,129},{129,65},{193,1... | collective-permute-start | bytes 442376 | tf_op jit(solution)/shard_map/ppermute | solution.py:300
  10.2 6.0 %collective-permute-start.5 = (bf16[144,512]{1,0:T(8,128)(2,1)S(1)}, bf16[144,512]{1,0:T(8,128)(2,1)S(1)}, u32[]{:S(2)}, u32[]{:S(2)}) collective-permute-start(bf16[144,512]{1,0:T(8,128)(2,1)S(1)} %collective-permute-done.4.b3), channel_id=1, source_target_pairs={{0,64},{64,0},{128,192},{192,128},{1,65},{65,1},{129,193},{193,129... | collective-permute-start | bytes 442376 | tf_op jit(solution)/shard_map/ppermute | solution.py:300
  19.3 11.0 %collective-permute-start.6 = (bf16[2,4,64,512]{3,2,1,0:T(8,128)(2,1)S(1)}, bf16[2,4,64,512]{3,2,1,0:T(8,128)(2,1)S(1)}, u32[]{:S(2)}, u32[]{:S(2)}) collective-permute-start(bf16[2,4,64,512]{3,2,1,0:T(8,128)(2,1)S(1)} %get-tuple-element.36), channel_id=1, source_target_pairs={{0,16},{4,20},{8,24},{12,28},{16,0},{20,4},{24,8},{28,12},{32,48},... | collective-permute-start | bytes 1572872 | tf_op jit(solution)/shard_map/ppermute | solution.py:305
  20.6 14.1 %collective-permute-start.10 = (bf16[2,4,64,512]{3,2,1,0:T(8,128)(2,1)S(1)}, bf16[2,4,64,512]{3,2,1,0:T(8,128)(2,1)S(1)}, u32[]{:S(2)}, u32[]{:S(2)}) collective-permute-start(bf16[2,4,64,512]{3,2,1,0:T(8,128)(2,1)S(1)} %get-tuple-element.38), channel_id=1, source_target_pairs={{0,48},{4,52},{8,56},{12,60},{16,32},{20,36},{24,40},{28,44},{32,1... | collective-permute-start | bytes 1572872 | tf_op jit(solution)/shard_map/ppermute | solution.py:305
  30.4 8.1 %collective-permute-start.7 = (bf16[4,64,512]{2,1,0:T(8,128)(2,1)S(1)}, bf16[4,64,512]{2,1,0:T(8,128)(2,1)S(1)}, u32[]{:S(2)}, u32[]{:S(2)}) collective-permute-start(bf16[4,64,512]{2,1,0:T(8,128)(2,1)S(1)} %fusion), channel_id=1, source_target_pairs={{0,48},{4,52},{8,56},{12,60},{16,32},{20,36},{24,40},{28,44},{32,1... | collective-permute-start | bytes 786440 | tf_op jit(solution)/shard_map/ppermute | solution.py:305
  34.8 7.0 %collective-permute-start.11 = (bf16[4,64,512]{2,1,0:T(8,128)(2,1)S(1)}, bf16[4,64,512]{2,1,0:T(8,128)(2,1)S(1)}, u32[]{:S(2)}, u32[]{:S(2)}) collective-permute-start(bf16[4,64,512]{2,1,0:T(8,128)(2,1)S(1)} %fusion.1), channel_id=1, source_target_pairs={{0,16},{4,20},{8,24},{12,28},{16,0},{20,4},{24,8},{28,12},{32,48},... | collective-permute-start | bytes 786440 | tf_op jit(solution)/shard_map/ppermute | solution.py:305
  38.5 9.2 %collective-permute-start.8 = (bf16[2,64,512]{2,1,0:T(8,128)(2,1)S(1)}, bf16[2,64,512]{2,1,0:T(8,128)(2,1)S(1)}, u32[]{:S(2)}, u32[]{:S(2)}) collective-permute-start(bf16[2,64,512]{2,1,0:T(8,128)(2,1)S(1)} %fusion.3), channel_id=1, source_target_pairs={{0,4},{4,0},{8,12},{12,8},{16,20},{20,16},{24,28},{28,24},{32,36},... | collective-permute-start | bytes 393224 | tf_op jit(solution)/shard_map/ppermute | solution.py:305
  41.9 10.4 %collective-permute-start.12 = (bf16[2,64,512]{2,1,0:T(8,128)(2,1)S(1)}, bf16[2,64,512]{2,1,0:T(8,128)(2,1)S(1)}, u32[]{:S(2)}, u32[]{:S(2)}) collective-permute-start(bf16[2,64,512]{2,1,0:T(8,128)(2,1)S(1)} %fusion.2), channel_id=1, source_target_pairs={{0,12},{4,8},{8,4},{12,0},{16,28},{20,24},{24,20},{28,16},{32,44},... | collective-permute-start | bytes 393224 | tf_op jit(solution)/shard_map/ppermute | solution.py:305
  47.8 7.3 %collective-permute-start.9 = (bf16[64,512]{1,0:T(8,128)(2,1)S(1)}, bf16[64,512]{1,0:T(8,128)(2,1)S(1)}, u32[]{:S(2)}, u32[]{:S(2)}) collective-permute-start(bf16[64,512]{1,0:T(8,128)(2,1)S(1)} %fusion.7), channel_id=1, source_target_pairs={{0,12},{4,8},{8,4},{12,0},{16,28},{20,24},{24,20},{28,16},{32,44},... | collective-permute-start | bytes 196616 | tf_op jit(solution)/shard_map/ppermute | solution.py:305
  52.4 5.3 %collective-permute-start.13 = (bf16[64,512]{1,0:T(8,128)(2,1)S(1)}, bf16[64,512]{1,0:T(8,128)(2,1)S(1)}, u32[]{:S(2)}, u32[]{:S(2)}) collective-permute-start(bf16[64,512]{1,0:T(8,128)(2,1)S(1)} %fusion.4), channel_id=1, source_target_pairs={{0,4},{4,0},{8,12},{12,8},{16,20},{20,16},{24,28},{28,24},{32,36},... | collective-permute-start | bytes 196616 | tf_op jit(solution)/shard_map/ppermute | solution.py:305
where the time goes:
time: 59.2 us; the launch traced here: 58.4 us
  starting transfers between devices  31.4 us (53%)
  waiting for transfers between devices  16.8 us (28%)
  Pallas kernels  8.94 us (15%)
  other arithmetic  1.07 us (2%)
    ppermute x8, starting transfers between devices, swap(): return lax.ppermute(value, 'head', pairs)  22.8 us
    ppermute x8, waiting for transfers between devices, swap(): return lax.ppermute(value, 'head', pairs)  15.1 us
    ppermute x6, starting transfers between devices, swap(): return lax.ppermute(value, 'ctx', pairs)  8.62 us
    pallas_call x1, Pallas kernels, mix_stage(): pl.pallas_call(mix_kernel, in_specs=[vmem] * 16, out_specs=[vmem] * 4, ou...  3.06 us
    pallas_call x1, Pallas kernels, fetch_stage(): pl.pallas_call(fetch_kernel, in_specs=[vmem] * 2 + [hbm] * 4, out_specs=[...  2.32 us
    pallas_call x1, Pallas kernels, local_stage(): pl.pallas_call(local_kernel, in_specs=[vmem] * 4 + [pl.BlockSpec(memory_s...  2.21 us
    ppermute x6, waiting for transfers between devices, swap(): return lax.ppermute(value, 'ctx', pairs)  1.67 us
    pallas_call x1, Pallas kernels, pack_stage(): pl.pallas_call(pack_kernel, in_specs=[hbm] * 7, out_specs=[vmem] * 6, out...  1.35 us
  transfers between devices with their start and end apart: 14, of which 7 were waited for; matrix products, arithmetic and copies ran while one was open for 1% of the time, Pallas kernels for 8%

commit v1 on v0

--- a/solution.py
+++ b/solution.py
@@ -16,8 +16,9 @@
 BF16 = jnp.bfloat16
 NEG = -1e30
 
-ORD_P = (0, 3, 1, 2)
-ORD_Q = (0, 1, 3, 2)
+STEPS = (4, 12, 1, 3)
+CHAINS = ((48, (0, 1, 2, 3)), (48, (1, 0, 3, 2)), (16, (2, 3, 0, 1)), (16, (3, 2, 1, 0)))
+CODES = [[(e >> (3 - r)) & 1 for r in range(4)] for e in range(15, -1, -1)]
 
 
 def pack_kernel(
@@ -88,9 +89,6 @@
     for load in loads:
         load.start()
     return loads
-
-
-CHUNKS = [(a, b) for a in (2, 1, 3, 0) for b in (2, 1, 3, 0)]
 
 
 def local_kernel(p_ref, rate_ref, res_ref, skip_ref, weight_hbm, base_ref, weight_ref, h_scr, wsems):
@@ -213,8 +211,9 @@
 
 def mix_kernel(
     a0, a1, a3, a2, b0, b1, b3, b2, base_ref, bias_ref, pull_ref, rate_ref, query_ref, gate_ref, w0, w1,
-    send_p, send_q, keep_p, keep_q, comb_scr,
+    *refs,
 ):
+    sends, keeps, comb_scr = refs[: len(CHAINS)], refs[len(CHAINS) : 2 * len(CHAINS)], refs[-1]
     rows, channels = query_ref.shape
     modes = rate_ref.shape[0]
     heads = channels // HD
@@ -262,22 +261,20 @@
         comb_scr[:, at] = (hyena + mixed / total).astype(BF16)
     comb = comb_scr[...]
     head = lax.axis_index("head")
-    my_y, my_z = head // NZ, head % NZ
-    for a, b in CHUNKS:
-        chunk = (my_y ^ a) * NZ + (my_z ^ b)
-        at = pl.ds(pl.multiple_of(chunk * channels, channels), channels)
-        half = channels // 2
+    half = channels // 2
+    for code in CODES:
+        mask = 0
+        for bit, step in zip(code, STEPS):
+            mask ^= bit * step
+        at = pl.ds(pl.multiple_of((head ^ mask) * channels, channels), channels)
         part = jnp.dot(comb[:, :half], w0[:, at], preferred_element_type=F32)
         part = part + jnp.dot(comb[:, half:], w1[:, at], preferred_element_type=F32)
-        for which, (send, keep) in enumerate(((send_p, keep_p), (send_q, keep_q))):
-            orders = ORD_P if which == 0 else ORD_Q
-            x = orders.index(a)
-            y = orders.index(b)
-            block = part[CH * which : CH * which + CH, :].astype(BF16)
-            if x < 2:
-                keep[x, y] = block
-            else:
-                send[x - 2, y] = block
+        start = 0
+        for (size, order), send, keep in zip(CHAINS, sends, keeps):
+            bits = [code[r] for r in order]
+            target = send if bits[0] else keep
+            target[4 * bits[1] + 2 * bits[2] + bits[3]] = part[start : start + size, :].astype(BF16)
+            start += size
 
 
 def mix_stage(first, second, base, bias, pull, rate, query, gate, w0, w1):
@@ -286,23 +283,20 @@
     return pl.pallas_call(
         mix_kernel,
         in_specs=[vmem] * 16,
-        out_specs=[vmem] * 4,
-        out_shape=[jax.ShapeDtypeStruct((2, 4, CH, channels), BF16)] * 4,
+        out_specs=[vmem] * (2 * len(CHAINS)),
+        out_shape=[jax.ShapeDtypeStruct((8, size, channels), BF16) for size, _ in CHAINS] * 2,
         scratch_shapes=[pltpu.VMEM((rows, channels), BF16)],
         compiler_params=pltpu.CompilerParams(vmem_limit_bytes=20 << 20),
         name="mix_project",
     )(*first, *second, base, bias, pull, rate, query, gate, w0, w1)
 
 
-def swap(value, axis, mask):
-    if axis == "ctx":
-        pairs = [(i, i ^ mask) for i in range(4)]
-        return lax.ppermute(value, "ctx", pairs)
-    if axis == "y":
-        pairs = [(y * NZ + z, (y ^ mask) * NZ + z) for y in range(NY) for z in range(NZ)]
-    else:
-        pairs = [(y * NZ + z, y * NZ + (z ^ mask)) for y in range(NY) for z in range(NZ)]
-    return lax.ppermute(value, "head", pairs)
+def swap(value, mask):
+    return lax.ppermute(value, "ctx", [(i, i ^ mask) for i in range(4)])
+
+
+def halve(value, step):
+    return lax.ppermute(value, "head", [(h, h ^ STEPS[step]) for h in range(NY * NZ)])
 
 
 def body(
@@ -321,18 +315,15 @@
         conv_in, value_in, modal_rate, key_proj, value_proj, modal_residue, skip
     )
 
-    def gather(value, mask):
-        return swap(value, "ctx", mask)
-
-    one_a = gather(own_a, 1)
-    three_b = gather(own_b, 3)
-    one_b = gather(own_b, 1)
-    three_a = gather(own_a, 3)
-    two_a = gather(one_a, 3)
-    two_b = gather(three_b, 1)
+    one_a = swap(own_a, 1)
+    three_b = swap(own_b, 3)
+    one_b = swap(own_b, 1)
+    three_a = swap(own_a, 3)
+    two_a = swap(one_a, 3)
+    two_b = swap(three_b, 1)
     base, w0 = local_stage(product, rate, residue, skip, out_weight)
     bias, pull, query, gate, w1 = fetch_stage(rate, residue, slots, query_proj, gate_in, out_weight)
-    send_p, send_q, keep_p, keep_q = mix_stage(
+    outs = mix_stage(
         (own_a, one_a, three_a, two_a), (own_b, one_b, three_b, two_b), base, bias, pull, rate, query, gate, w0, w1
     )
 
@@ -342,19 +333,16 @@
             result = result + term.astype(F32)
         return result.astype(BF16)
 
-    keeps = (keep_p, keep_q)
-    plans = ((("y", 1), ("y", 3), ("z", 1), ("z", 3)), (("y", 3), ("y", 1), ("z", 3), ("z", 1)))
-    first = [swap(send, *plan[0]) for send, plan in zip((send_p, send_q), plans)]
-    second = [swap(total(k[1], a[1]), *plan[1]) for k, a, plan in zip(keeps, first, plans)]
-    third = [swap(total(k[0, 2:], a[0, 2:], b[2:]), *plan[2]) for k, a, b, plan in zip(keeps, first, second, plans)]
-    fourth = [
-        swap(total(k[0, 1], a[0, 1], b[1], c[1]), *plan[3])
-        for k, a, b, c, plan in zip(keeps, first, second, third, plans)
-    ]
-    parts = [
-        total(k[0, 0], a[0, 0], b[0], c[0], d) for k, a, b, c, d in zip(keeps, first, second, third, fourth)
-    ]
-    return jnp.concatenate(parts, axis=0)
+    count = len(CHAINS)
+    sends, keeps, got = list(outs[:count]), outs[count:], [[] for _ in CHAINS]
+    for r in range(4):
+        for c in range(count):
+            got[c].append(halve(sends[c], CHAINS[c][1][r]))
+        size = 8 >> (r + 1)
+        for c in range(count):
+            terms = [keeps[c]] + got[c]
+            sends[c] = total(*[t[size : 2 * size] if r < 3 else t[0] for t in terms])
+    return jnp.concatenate(sends, axis=0)
 
 
 def solution(mesh):

time: 59.2 us -> 70.7 us (1.19)
  starting transfers between devices: 31.4 us -> 41.2 us
  waiting for transfers between devices: 16.8 us -> 18.4 us
    ppermute x14 -> x22, starting transfers between devices: 31.4 us -> 41.2 us  [the longest x16 32.6 us: halve(): lax.ppermute(value, 'head', [(h, h ^ STEPS[step]) for h in range(NY * NZ)])]
    ppermute x14 -> x22, waiting for transfers between devices: 16.8 us -> 18.4 us  [the longest x16 16.7 us: halve(): lax.ppermute(value, 'head', [(h, h ^ STEPS[step]) for h in range(NY * NZ)])]
  transfers between devices with their start and end apart: 14 -> 22, of which waited for: 7 -> 11; matrix products, arithmetic and copies ran while one was open for 1% -> 1% of each run, Pallas kernels for 8% -> 6%
where the time goes in v1:
time: 70.7 us; the launch traced here: 69.8 us
  starting transfers between devices  41.2 us (58%)
  waiting for transfers between devices  18.4 us (26%)
  Pallas kernels  8.96 us (13%)
  other arithmetic  1.1 us (2%)
    ppermute x16, starting transfers between devices, halve(): lax.ppermute(value, 'head', [(h, h ^ STEPS[step]) for h in range(NY * NZ)])  32.6 us
    ppermute x16, waiting for transfers between devices, halve(): lax.ppermute(value, 'head', [(h, h ^ STEPS[step]) for h in range(NY * NZ)])  16.7 us
    ppermute x6, starting transfers between devices, swap(): return lax.ppermute(value, 'ctx', [(i, i ^ mask) for i in range(4)])  8.62 us
    pallas_call x1, Pallas kernels, mix_stage(): pl.pallas_call(mix_kernel, in_specs=[vmem] * 16, out_specs=[vmem] * (2 *...  3.08 us
    pallas_call x1, Pallas kernels, fetch_stage(): pl.pallas_call(fetch_kernel, in_specs=[vmem] * 2 + [hbm] * 4, out_specs=[...  2.32 us
    pallas_call x1, Pallas kernels, local_stage(): pl.pallas_call(local_kernel, in_specs=[vmem] * 4 + [pl.BlockSpec(memory_s...  2.21 us
    ppermute x6, waiting for transfers between devices, swap(): return lax.ppermute(value, 'ctx', [(i, i ^ mask) for i in range(4)])  1.67 us
  transfers between devices with their start and end apart: 22, of which 11 were waited for; matrix products, arithmetic and copies ran while one was open for 1% of the time, Pallas kernels for 6%

profile of v1, /device:TPU:2, one launch (start us, length us, event | category | flops | bytes accessed | tf_op | source)
XLA Modules:
  0.0 69.8 jit_solution(2539537536049496119)
XLA Ops:
  1.4 2.3 %collective-permute-start = (bf16[144,512]{1,0:T(8,128)(2,1)S(1)}, bf16[144,512]{1,0:T(8,128)(2,1)S(1)}, u32[]{:S(2)}, u32[]{:S(2)}) collective-permute-start(bf16[144,512]{1,0:T(8,128)(2,1)S(1)} %get-tuple-element.26.a0), channel_id=1, source_target_pairs={{0,64},{64,0},{128,192},{192,128},{1,65},{65,1},{129,193},{193,129... | collective-permute-start | bytes 442376 | tf_op jit(solution)/shard_map/ppermute | solution.py:295
  4.1 1.6 %collective-permute-start.1 = (bf16[144,512]{1,0:T(8,128)(2,1)S(1)}, bf16[144,512]{1,0:T(8,128)(2,1)S(1)}, u32[]{:S(2)}, u32[]{:S(2)}) collective-permute-start(bf16[144,512]{1,0:T(8,128)(2,1)S(1)} %get-tuple-element.26.a0), channel_id=1, source_target_pairs={{0,192},{64,128},{128,64},{192,0},{1,193},{65,129},{129,65},{193,1... | collective-permute-start | bytes 442376 | tf_op jit(solution)/shard_map/ppermute | solution.py:295
  7.5 1.5 %collective-permute-start.2 = (bf16[144,512]{1,0:T(8,128)(2,1)S(1)}, bf16[144,512]{1,0:T(8,128)(2,1)S(1)}, u32[]{:S(2)}, u32[]{:S(2)}) collective-permute-start(bf16[144,512]{1,0:T(8,128)(2,1)S(1)} %collective-permute-done.a1), channel_id=1, source_target_pairs={{0,192},{64,128},{128,64},{192,0},{1,193},{65,129},{129,65},{193,1... | collective-permute-start | bytes 442376 | tf_op jit(solution)/shard_map/ppermute | solution.py:295
  10.2 1.5 %collective-permute-start.5 = (bf16[144,512]{1,0:T(8,128)(2,1)S(1)}, bf16[144,512]{1,0:T(8,128)(2,1)S(1)}, u32[]{:S(2)}, u32[]{:S(2)}) collective-permute-start(bf16[144,512]{1,0:T(8,128)(2,1)S(1)} %collective-permute-done.4.b3), channel_id=1, source_target_pairs={{0,64},{64,0},{128,192},{192,128},{1,65},{65,1},{129,193},{193,129... | collective-permute-start | bytes 442376 | tf_op jit(solution)/shard_map/ppermute | solution.py:295
  11.6 2.2 %local_conv.1 = (f32[128,512]{1,0:T(8,128)S(1)}, bf16[256,8192]{1,0:T(8,128)(2,1)S(1)}) custom-call(f32[128,512]{1,0:T(8,128)S(1)} %get-tuple-element.28.p_ref, f32[16,512]{1,0:T(8,128)S(1)} %get-tuple-element.29.rate_ref, f32[16,512]{1,0:T(8,128)S(1)} %get-tuple-element.30.res_ref, f32[1,512]{1,0:T(1,128)S(1)} %get-tuple-element.31.skip_ref, ...), custom_call_target="tpu_custom_call" | custom-call | tf_op jit(solution)/shard_map/local_conv/pallas_call | solution.py:142
  13.9 2.3 %fetch_weight.1 = (f32[4,128,128]{2,1,0:T(8,128)S(1)}, f32[2,8,16,512]{3,2,1,0:T(8,128)S(1)}, bf16[128,512]{1,0:T(8,128)(2,1)S(1)}, bf16[128,512]{1,0:T(8,128)(2,1)S(1)}, bf16[256,8192]{1,0:T(8,128)(2,1)S(1)}) custom-call(f32[16,512]{1,0:T(8,128)S(1)} %get-tuple-element.29.rate_ref, f32[16,512]{1,0:T(8,128)S(1)} %get-tuple-element.30.res_ref, s32[8]{0:T(128)} %slot_hbm.1, ...), custom_call_target="tpu_custom_call" | custom-call | tf_op jit(solution)/shard_map/fetch_weight/pallas_call | solution.py:191
  16.2 3.1 %mix_project.1 = (bf16[8,48,512]{2,1,0:T(8,128)(2,1)S(1)}, bf16[8,48,512]{2,1,0:T(8,128)(2,1)S(1)}, bf16[8,16,512]{2,1,0:T(8,128)(2,1)S(1)}, bf16[8,16,512]{2,1,...) custom-call(bf16[144,512]{1,0:T(8,128)(2,1)S(1)} %get-tuple-element., ...), custom_call_target="tpu_custom_call" | custom-call | tf_op jit(solution)/shard_map/mix_project/pallas_call | solution.py:283
  19.3 3.1 %collective-permute-start.14 = (bf16[8,16,512]{2,1,0:T(8,128)(2,1)S(1)}, bf16[8,16,512]{2,1,0:T(8,128)(2,1)S(1)}, u32[]{:S(2)}, u32[]{:S(2)}) collective-permute-start(bf16[8,16,512]{2,1,0:T(8,128)(2,1)S(1)} %get-tuple-element.44), channel_id=1, source_target_pairs={{0,4},{4,0},{8,12},{12,8},{16,20},{20,16},{24,28},{28,24},{32,36},... | collective-permute-start | bytes 393224 | tf_op jit(solution)/shard_map/ppermute | solution.py:299
  22.4 4.5 %collective-permute-start.18 = (bf16[8,16,512]{2,1,0:T(8,128)(2,1)S(1)}, bf16[8,16,512]{2,1,0:T(8,128)(2,1)S(1)}, u32[]{:S(2)}, u32[]{:S(2)}) collective-permute-start(bf16[8,16,512]{2,1,0:T(8,128)(2,1)S(1)} %get-tuple-element.46), channel_id=1, source_target_pairs={{0,12},{4,8},{8,4},{12,0},{16,28},{20,24},{24,20},{28,16},{32,44},... | collective-permute-start | bytes 393224 | tf_op jit(solution)/shard_map/ppermute | solution.py:299
  26.8 1.6 %collective-permute-start.6 = (bf16[8,48,512]{2,1,0:T(8,128)(2,1)S(1)}, bf16[8,48,512]{2,1,0:T(8,128)(2,1)S(1)}, u32[]{:S(2)}, u32[]{:S(2)}) collective-permute-start(bf16[8,48,512]{2,1,0:T(8,128)(2,1)S(1)} %get-tuple-element.40), channel_id=1, source_target_pairs={{0,16},{4,20},{8,24},{12,28},{16,0},{20,4},{24,8},{28,12},{32,48},... | collective-permute-start | bytes 1179656 | tf_op jit(solution)/shard_map/ppermute | solution.py:299
  28.4 2.2 %collective-permute-start.10 = (bf16[8,48,512]{2,1,0:T(8,128)(2,1)S(1)}, bf16[8,48,512]{2,1,0:T(8,128)(2,1)S(1)}, u32[]{:S(2)}, u32[]{:S(2)}) collective-permute-start(bf16[8,48,512]{2,1,0:T(8,128)(2,1)S(1)} %get-tuple-element.42), channel_id=1, source_target_pairs={{0,48},{4,52},{8,56},{12,60},{16,32},{20,36},{24,40},{28,44},{32,1... | collective-permute-start | bytes 1179656 | tf_op jit(solution)/shard_map/ppermute | solution.py:299
  30.6 1.6 %collective-permute-start.15 = (bf16[4,16,512]{2,1,0:T(8,128)(2,1)S(1)}, bf16[4,16,512]{2,1,0:T(8,128)(2,1)S(1)}, u32[]{:S(2)}, u32[]{:S(2)}) collective-permute-start(bf16[4,16,512]{2,1,0:T(8,128)(2,1)S(1)} %add_convert_fusion.5), channel_id=1, source_target_pairs={{0,12},{4,8},{8,4},{12,0},{16,28},{20,24},{24,20},{28,16},{32,44},... | collective-permute-start | bytes 196616 | tf_op jit(solution)/shard_map/ppermute | solution.py:299
  32.2 2.0 %collective-permute-start.19 = (bf16[4,16,512]{2,1,0:T(8,128)(2,1)S(1)}, bf16[4,16,512]{2,1,0:T(8,128)(2,1)S(1)}, u32[]{:S(2)}, u32[]{:S(2)}) collective-permute-start(bf16[4,16,512]{2,1,0:T(8,128)(2,1)S(1)} %add_convert_fusion.4), channel_id=1, source_target_pairs={{0,4},{4,0},{8,12},{12,8},{16,20},{20,16},{24,28},{28,24},{32,36},... | collective-permute-start | bytes 196616 | tf_op jit(solution)/shard_map/ppermute | solution.py:299
  34.2 2.9 %collective-permute-done.15 = bf16[4,16,512]{2,1,0:T(8,128)(2,1)S(1)} collective-permute-done((bf16[4,16,512]{2,1,0:T(8,128)(2,1)S(1)}, bf16[4,16,512]{2,1,0:T(8,128)(2,1)S(1)}, u32[]{:S(2)}, u32[]{:S(2)}) %collective-permute-start.15) | collective-permute-done | bytes 65568 | tf_op jit(solution)/shard_map/ppermute | solution.py:299
  38.0 2.6 %collective-permute-start.20 = (bf16[2,16,512]{2,1,0:T(8,128)(2,1)S(1)}, bf16[2,16,512]{2,1,0:T(8,128)(2,1)S(1)}, u32[]{:S(2)}, u32[]{:S(2)}) collective-permute-start(bf16[2,16,512]{2,1,0:T(8,128)(2,1)S(1)} %add_convert_fusion.10), channel_id=1, source_target_pairs={{0,48},{4,52},{8,56},{12,60},{16,32},{20,36},{24,40},{28,44},{32,1... | collective-permute-start | bytes 98312 | tf_op jit(solution)/shard_map/ppermute | solution.py:299
  43.5 3.3 %collective-permute-done.17 = bf16[1,16,512]{2,1,0:T(8,128)(2,1)S(1)} collective-permute-done((bf16[1,16,512]{2,1,0:T(8,128)(2,1)S(1)}, bf16[1,16,512]{2,1,0:T(8,128)(2,1)S(1)}, u32[]{:S(2)}, u32[]{:S(2)}) %collective-permute-start.17) | collective-permute-done | bytes 16416 | tf_op jit(solution)/shard_map/ppermute | solution.py:299
  47.3 2.5 %collective-permute-start.7 = (bf16[4,48,512]{2,1,0:T(8,128)(2,1)S(1)}, bf16[4,48,512]{2,1,0:T(8,128)(2,1)S(1)}, u32[]{:S(2)}, u32[]{:S(2)}) collective-permute-start(bf16[4,48,512]{2,1,0:T(8,128)(2,1)S(1)} %add_convert_fusion.1), channel_id=1, source_target_pairs={{0,48},{4,52},{8,56},{12,60},{16,32},{20,36},{24,40},{28,44},{32,1... | collective-permute-start | bytes 589832 | tf_op jit(solution)/shard_map/ppermute | solution.py:299
  49.9 4.3 %collective-permute-done.7 = bf16[4,48,512]{2,1,0:T(8,128)(2,1)S(1)} collective-permute-done((bf16[4,48,512]{2,1,0:T(8,128)(2,1)S(1)}, bf16[4,48,512]{2,1,0:T(8,128)(2,1)S(1)}, u32[]{:S(2)}, u32[]{:S(2)}) %collective-permute-start.7) | collective-permute-done | bytes 196640 | tf_op jit(solution)/shard_map/ppermute | solution.py:299
  54.3 2.2 %collective-permute-start.8 = (bf16[2,48,512]{2,1,0:T(8,128)(2,1)S(1)}, bf16[2,48,512]{2,1,0:T(8,128)(2,1)S(1)}, u32[]{:S(2)}, u32[]{:S(2)}) collective-permute-start(bf16[2,48,512]{2,1,0:T(8,128)(2,1)S(1)} %add_convert_fusion.3), channel_id=1, source_target_pairs={{0,4},{4,0},{8,12},{12,8},{16,20},{20,16},{24,28},{28,24},{32,36},... | collective-permute-start | bytes 294920 | tf_op jit(solution)/shard_map/ppermute | solution.py:299
  56.5 3.6 %collective-permute-start.12 = (bf16[2,48,512]{2,1,0:T(8,128)(2,1)S(1)}, bf16[2,48,512]{2,1,0:T(8,128)(2,1)S(1)}, u32[]{:S(2)}, u32[]{:S(2)}) collective-permute-start(bf16[2,48,512]{2,1,0:T(8,128)(2,1)S(1)} %add_convert_fusion.2), channel_id=1, source_target_pairs={{0,12},{4,8},{8,4},{12,0},{16,28},{20,24},{24,20},{28,16},{32,44},... | collective-permute-start | bytes 294920 | tf_op jit(solution)/shard_map/ppermute | solution.py:299
  60.1 1.7 %collective-permute-done.8 = bf16[2,48,512]{2,1,0:T(8,128)(2,1)S(1)} collective-permute-done((bf16[2,48,512]{2,1,0:T(8,128)(2,1)S(1)}, bf16[2,48,512]{2,1,0:T(8,128)(2,1)S(1)}, u32[]{:S(2)}, u32[]{:S(2)}) %collective-permute-start.8) | collective-permute-done | bytes 98336 | tf_op jit(solution)/shard_map/ppermute | solution.py:299
  61.9 2.1 %collective-permute-start.9 = (bf16[1,48,512]{2,1,0:T(8,128)(2,1)S(1)}, bf16[1,48,512]{2,1,0:T(8,128)(2,1)S(1)}, u32[]{:S(2)}, u32[]{:S(2)}) collective-permute-start(bf16[1,48,512]{2,1,0:T(8,128)(2,1)S(1)} %add_convert_fusion.9), channel_id=1, source_target_pairs={{0,12},{4,8},{8,4},{12,0},{16,28},{20,24},{24,20},{28,16},{32,44},... | collective-permute-start | bytes 147464 | tf_op jit(solution)/shard_map/ppermute | solution.py:299
  64.0 2.5 %collective-permute-start.13 = (bf16[1,48,512]{2,1,0:T(8,128)(2,1)S(1)}, bf16[1,48,512]{2,1,0:T(8,128)(2,1)S(1)}, u32[]{:S(2)}, u32[]{:S(2)}) collective-permute-start(bf16[1,48,512]{2,1,0:T(8,128)(2,1)S(1)} %add_convert_fusion.8), channel_id=1, source_target_pairs={{0,4},{4,0},{8,12},{12,8},{16,20},{20,16},{24,28},{28,24},{32,36},... | collective-permute-start | bytes 147464 | tf_op jit(solution)/shard_map/ppermute | solution.py:299
  66.6 1.6 %collective-permute-done.9 = bf16[1,48,512]{2,1,0:T(8,128)(2,1)S(1)} collective-permute-done((bf16[1,48,512]{2,1,0:T(8,128)(2,1)S(1)}, bf16[1,48,512]{2,1,0:T(8,128)(2,1)S(1)}, u32[]{:S(2)}, u32[]{:S(2)}) %collective-permute-start.9) | collective-permute-done | bytes 49184 | tf_op jit(solution)/shard_map/ppermute | solution.py:299
  (41 shorter events, 10.9 us)
Async XLA Ops:
  1.4 6.2 %collective-permute-start = (bf16[144,512]{1,0:T(8,128)(2,1)S(1)}, bf16[144,512]{1,0:T(8,128)(2,1)S(1)}, u32[]{:S(2)}, u32[]{:S(2)}) collective-permute-start(bf16[144,512]{1,0:T(8,128)(2,1)S(1)} %get-tuple-element.26.a0), channel_id=1, source_target_pairs={{0,64},{64,0},{128,192},{192,128},{1,65},{65,1},{129,193},{193,129... | collective-permute-start | bytes 442376 | tf_op jit(solution)/shard_map/ppermute | solution.py:295
  3.7 6.5 %collective-permute-start.4 = (bf16[144,512]{1,0:T(8,128)(2,1)S(1)}, bf16[144,512]{1,0:T(8,128)(2,1)S(1)}, u32[]{:S(2)}, u32[]{:S(2)}) collective-permute-start(bf16[144,512]{1,0:T(8,128)(2,1)S(1)} %get-tuple-element.27.b0), channel_id=1, source_target_pairs={{0,192},{64,128},{128,64},{192,0},{1,193},{65,129},{129,65},{193,1... | collective-permute-start | bytes 442376 | tf_op jit(solution)/shard_map/ppermute | solution.py:295
  4.1 12.0 %collective-permute-start.1 = (bf16[144,512]{1,0:T(8,128)(2,1)S(1)}, bf16[144,512]{1,0:T(8,128)(2,1)S(1)}, u32[]{:S(2)}, u32[]{:S(2)}) collective-permute-start(bf16[144,512]{1,0:T(8,128)(2,1)S(1)} %get-tuple-element.26.a0), channel_id=1, source_target_pairs={{0,192},{64,128},{128,64},{192,0},{1,193},{65,129},{129,65},{193,1... | collective-permute-start | bytes 442376 | tf_op jit(solution)/shard_map/ppermute | solution.py:295
  5.7 10.5 %collective-permute-start.3 = (bf16[144,512]{1,0:T(8,128)(2,1)S(1)}, bf16[144,512]{1,0:T(8,128)(2,1)S(1)}, u32[]{:S(2)}, u32[]{:S(2)}) collective-permute-start(bf16[144,512]{1,0:T(8,128)(2,1)S(1)} %get-tuple-element.27.b0), channel_id=1, source_target_pairs={{0,64},{64,0},{128,192},{192,128},{1,65},{65,1},{129,193},{193,129... | collective-permute-start | bytes 442376 | tf_op jit(solution)/shard_map/ppermute | solution.py:295
  7.5 8.7 %collective-permute-start.2 = (bf16[144,512]{1,0:T(8,128)(2,1)S(1)}, bf16[144,512]{1,0:T(8,128)(2,1)S(1)}, u32[]{:S(2)}, u32[]{:S(2)}) collective-permute-start(bf16[144,512]{1,0:T(8,128)(2,1)S(1)} %collective-permute-done.a1), channel_id=1, source_target_pairs={{0,192},{64,128},{128,64},{192,0},{1,193},{65,129},{129,65},{193,1... | collective-permute-start | bytes 442376 | tf_op jit(solution)/shard_map/ppermute | solution.py:295
  10.2 6.0 %collective-permute-start.5 = (bf16[144,512]{1,0:T(8,128)(2,1)S(1)}, bf16[144,512]{1,0:T(8,128)(2,1)S(1)}, u32[]{:S(2)}, u32[]{:S(2)}) collective-permute-start(bf16[144,512]{1,0:T(8,128)(2,1)S(1)} %collective-permute-done.4.b3), channel_id=1, source_target_pairs={{0,64},{64,0},{128,192},{192,128},{1,65},{65,1},{129,193},{193,129... | collective-permute-start | bytes 442376 | tf_op jit(solution)/shard_map/ppermute | solution.py:295
  19.3 11.3 %collective-permute-start.14 = (bf16[8,16,512]{2,1,0:T(8,128)(2,1)S(1)}, bf16[8,16,512]{2,1,0:T(8,128)(2,1)S(1)}, u32[]{:S(2)}, u32[]{:S(2)}) collective-permute-start(bf16[8,16,512]{2,1,0:T(8,128)(2,1)S(1)} %get-tuple-element.44), channel_id=1, source_target_pairs={{0,4},{4,0},{8,12},{12,8},{16,20},{20,16},{24,28},{28,24},{32,36},... | collective-permute-start | bytes 393224 | tf_op jit(solution)/shard_map/ppermute | solution.py:299
  22.4 9.9 %collective-permute-start.18 = (bf16[8,16,512]{2,1,0:T(8,128)(2,1)S(1)}, bf16[8,16,512]{2,1,0:T(8,128)(2,1)S(1)}, u32[]{:S(2)}, u32[]{:S(2)}) collective-permute-start(bf16[8,16,512]{2,1,0:T(8,128)(2,1)S(1)} %get-tuple-element.46), channel_id=1, source_target_pairs={{0,12},{4,8},{8,4},{12,0},{16,28},{20,24},{24,20},{28,16},{32,44},... | collective-permute-start | bytes 393224 | tf_op jit(solution)/shard_map/ppermute | solution.py:299
  26.8 20.4 %collective-permute-start.6 = (bf16[8,48,512]{2,1,0:T(8,128)(2,1)S(1)}, bf16[8,48,512]{2,1,0:T(8,128)(2,1)S(1)}, u32[]{:S(2)}, u32[]{:S(2)}) collective-permute-start(bf16[8,48,512]{2,1,0:T(8,128)(2,1)S(1)} %get-tuple-element.40), channel_id=1, source_target_pairs={{0,16},{4,20},{8,24},{12,28},{16,0},{20,4},{24,8},{28,12},{32,48},... | collective-permute-start | bytes 1179656 | tf_op jit(solution)/shard_map/ppermute | solution.py:299
  28.4 21.4 %collective-permute-start.10 = (bf16[8,48,512]{2,1,0:T(8,128)(2,1)S(1)}, bf16[8,48,512]{2,1,0:T(8,128)(2,1)S(1)}, u32[]{:S(2)}, u32[]{:S(2)}) collective-permute-start(bf16[8,48,512]{2,1,0:T(8,128)(2,1)S(1)} %get-tuple-element.42), channel_id=1, source_target_pairs={{0,48},{4,52},{8,56},{12,60},{16,32},{20,36},{24,40},{28,44},{32,1... | collective-permute-start | bytes 1179656 | tf_op jit(solution)/shard_map/ppermute | solution.py:299
  30.6 6.6 %collective-permute-start.15 = (bf16[4,16,512]{2,1,0:T(8,128)(2,1)S(1)}, bf16[4,16,512]{2,1,0:T(8,128)(2,1)S(1)}, u32[]{:S(2)}, u32[]{:S(2)}) collective-permute-start(bf16[4,16,512]{2,1,0:T(8,128)(2,1)S(1)} %add_convert_fusion.5), channel_id=1, source_target_pairs={{0,12},{4,8},{8,4},{12,0},{16,28},{20,24},{24,20},{28,16},{32,44},... | collective-permute-start | bytes 196616 | tf_op jit(solution)/shard_map/ppermute | solution.py:299
  32.2 5.7 %collective-permute-start.19 = (bf16[4,16,512]{2,1,0:T(8,128)(2,1)S(1)}, bf16[4,16,512]{2,1,0:T(8,128)(2,1)S(1)}, u32[]{:S(2)}, u32[]{:S(2)}) collective-permute-start(bf16[4,16,512]{2,1,0:T(8,128)(2,1)S(1)} %add_convert_fusion.4), channel_id=1, source_target_pairs={{0,4},{4,0},{8,12},{12,8},{16,20},{20,16},{24,28},{28,24},{32,36},... | collective-permute-start | bytes 196616 | tf_op jit(solution)/shard_map/ppermute | solution.py:299
  37.2 4.2 %collective-permute-start.16 = (bf16[2,16,512]{2,1,0:T(8,128)(2,1)S(1)}, bf16[2,16,512]{2,1,0:T(8,128)(2,1)S(1)}, u32[]{:S(2)}, u32[]{:S(2)}) collective-permute-start(bf16[2,16,512]{2,1,0:T(8,128)(2,1)S(1)} %add_convert_fusion.11), channel_id=1, source_target_pairs={{0,16},{4,20},{8,24},{12,28},{16,0},{20,4},{24,8},{28,12},{32,48},... | collective-permute-start | bytes 98312 | tf_op jit(solution)/shard_map/ppermute | solution.py:299
  38.0 5.2 %collective-permute-start.20 = (bf16[2,16,512]{2,1,0:T(8,128)(2,1)S(1)}, bf16[2,16,512]{2,1,0:T(8,128)(2,1)S(1)}, u32[]{:S(2)}, u32[]{:S(2)}) collective-permute-start(bf16[2,16,512]{2,1,0:T(8,128)(2,1)S(1)} %add_convert_fusion.10), channel_id=1, source_target_pairs={{0,48},{4,52},{8,56},{12,60},{16,32},{20,36},{24,40},{28,44},{32,1... | collective-permute-start | bytes 98312 | tf_op jit(solution)/shard_map/ppermute | solution.py:299
  41.4 5.4 %collective-permute-start.17 = (bf16[1,16,512]{2,1,0:T(8,128)(2,1)S(1)}, bf16[1,16,512]{2,1,0:T(8,128)(2,1)S(1)}, u32[]{:S(2)}, u32[]{:S(2)}) collective-permute-start(bf16[1,16,512]{2,1,0:T(8,128)(2,1)S(1)} %add_convert_fusion.15), channel_id=1, source_target_pairs={{0,48},{4,52},{8,56},{12,60},{16,32},{20,36},{24,40},{28,44},{32,1... | collective-permute-start | bytes 49160 | tf_op jit(solution)/shard_map/ppermute | solution.py:299
  43.2 4.0 %collective-permute-start.21 = (bf16[1,16,512]{2,1,0:T(8,128)(2,1)S(1)}, bf16[1,16,512]{2,1,0:T(8,128)(2,1)S(1)}, u32[]{:S(2)}, u32[]{:S(2)}) collective-permute-start(bf16[1,16,512]{2,1,0:T(8,128)(2,1)S(1)} %add_convert_fusion.14), channel_id=1, source_target_pairs={{0,16},{4,20},{8,24},{12,28},{16,0},{20,4},{24,8},{28,12},{32,48},... | collective-permute-start | bytes 49160 | tf_op jit(solution)/shard_map/ppermute | solution.py:299
  47.3 7.0 %collective-permute-start.7 = (bf16[4,48,512]{2,1,0:T(8,128)(2,1)S(1)}, bf16[4,48,512]{2,1,0:T(8,128)(2,1)S(1)}, u32[]{:S(2)}, u32[]{:S(2)}) collective-permute-start(bf16[4,48,512]{2,1,0:T(8,128)(2,1)S(1)} %add_convert_fusion.1), channel_id=1, source_target_pairs={{0,48},{4,52},{8,56},{12,60},{16,32},{20,36},{24,40},{28,44},{32,1... | collective-permute-start | bytes 589832 | tf_op jit(solution)/shard_map/ppermute | solution.py:299
  49.8 6.7 %collective-permute-start.11 = (bf16[4,48,512]{2,1,0:T(8,128)(2,1)S(1)}, bf16[4,48,512]{2,1,0:T(8,128)(2,1)S(1)}, u32[]{:S(2)}, u32[]{:S(2)}) collective-permute-start(bf16[4,48,512]{2,1,0:T(8,128)(2,1)S(1)} %add_convert_fusion), channel_id=1, source_target_pairs={{0,16},{4,20},{8,24},{12,28},{16,0},{20,4},{24,8},{28,12},{32,48},... | collective-permute-start | bytes 589832 | tf_op jit(solution)/shard_map/ppermute | solution.py:299
  54.3 7.5 %collective-permute-start.8 = (bf16[2,48,512]{2,1,0:T(8,128)(2,1)S(1)}, bf16[2,48,512]{2,1,0:T(8,128)(2,1)S(1)}, u32[]{:S(2)}, u32[]{:S(2)}) collective-permute-start(bf16[2,48,512]{2,1,0:T(8,128)(2,1)S(1)} %add_convert_fusion.3), channel_id=1, source_target_pairs={{0,4},{4,0},{8,12},{12,8},{16,20},{20,16},{24,28},{28,24},{32,36},... | collective-permute-start | bytes 294920 | tf_op jit(solution)/shard_map/ppermute | solution.py:299
  56.5 7.5 %collective-permute-start.12 = (bf16[2,48,512]{2,1,0:T(8,128)(2,1)S(1)}, bf16[2,48,512]{2,1,0:T(8,128)(2,1)S(1)}, u32[]{:S(2)}, u32[]{:S(2)}) collective-permute-start(bf16[2,48,512]{2,1,0:T(8,128)(2,1)S(1)} %add_convert_fusion.2), channel_id=1, source_target_pairs={{0,12},{4,8},{8,4},{12,0},{16,28},{20,24},{24,20},{28,16},{32,44},... | collective-permute-start | bytes 294920 | tf_op jit(solution)/shard_map/ppermute | solution.py:299
  61.9 6.3 %collective-permute-start.9 = (bf16[1,48,512]{2,1,0:T(8,128)(2,1)S(1)}, bf16[1,48,512]{2,1,0:T(8,128)(2,1)S(1)}, u32[]{:S(2)}, u32[]{:S(2)}) collective-permute-start(bf16[1,48,512]{2,1,0:T(8,128)(2,1)S(1)} %add_convert_fusion.9), channel_id=1, source_target_pairs={{0,12},{4,8},{8,4},{12,0},{16,28},{20,24},{24,20},{28,16},{32,44},... | collective-permute-start | bytes 147464 | tf_op jit(solution)/shard_map/ppermute | solution.py:299
  64.0 5.1 %collective-permute-start.13 = (bf16[1,48,512]{2,1,0:T(8,128)(2,1)S(1)}, bf16[1,48,512]{2,1,0:T(8,128)(2,1)S(1)}, u32[]{:S(2)}, u32[]{:S(2)}) collective-permute-start(bf16[1,48,512]{2,1,0:T(8,128)(2,1)S(1)} %add_convert_fusion.8), channel_id=1, source_target_pairs={{0,4},{4,0},{8,12},{12,8},{16,20},{20,16},{24,28},{28,24},{32,36},... | collective-permute-start | bytes 147464 | tf_op jit(solution)/shard_map/ppermute | solution.py:299

commit v2 on v1

--- a/solution.py
+++ b/solution.py
@@ -291,6 +291,28 @@
     )(*first, *second, base, bias, pull, rate, query, gate, w0, w1)
 
 
+def last_kernel(*refs):
+    start = 0
+    for c, (size, _) in enumerate(CHAINS):
+        result = refs[5 * c][0].astype(F32)
+        for ref in refs[5 * c + 1 : 5 * c + 5]:
+            result = result + ref[0].astype(F32)
+        refs[-1][start : start + size, :] = result.astype(BF16)
+        start += size
+
+
+def last_stage(terms, rows, channels):
+    vmem = pl.BlockSpec(memory_space=pltpu.VMEM)
+    return pl.pallas_call(
+        last_kernel,
+        in_specs=[vmem] * len(terms),
+        out_specs=vmem,
+        out_shape=jax.ShapeDtypeStruct((rows, channels), BF16),
+        compiler_params=pltpu.CompilerParams(vmem_limit_bytes=4 << 20),
+        name="last_sum",
+    )(*terms)
+
+
 def swap(value, mask):
     return lax.ppermute(value, "ctx", [(i, i ^ mask) for i in range(4)])
 
@@ -339,10 +361,13 @@
         for c in range(count):
             got[c].append(halve(sends[c], CHAINS[c][1][r]))
         size = 8 >> (r + 1)
+        if r == 3:
+            break
         for c in range(count):
             terms = [keeps[c]] + got[c]
-            sends[c] = total(*[t[size : 2 * size] if r < 3 else t[0] for t in terms])
-    return jnp.concatenate(sends, axis=0)
+            sends[c] = total(*[t[size : 2 * size] for t in terms])
+    terms = [term for c in range(count) for term in [keeps[c]] + got[c]]
+    return last_stage(terms, *query_proj.shape)
 
 
 def solution(mesh):

time: 70.7 us -> 67.6 us (0.956); the launches traced: 69.8 us -> 67.5 us
  waiting for transfers between devices: 18.4 us -> 13.5 us
  starting transfers between devices: 41.2 us -> 43.9 us
  other arithmetic: 1.1 us -> 0.34 us
  Pallas kernels: 8.96 us -> 9.7 us
    ppermute x16, waiting for transfers between devices: 16.7 us -> 11.8 us  [halve(): lax.ppermute(value, 'head', [(h, h ^ STEPS[step]) for h in range(NY * NZ)])]
    ppermute x16, starting transfers between devices: 32.6 us -> 35.2 us  [halve(): lax.ppermute(value, 'head', [(h, h ^ STEPS[step]) for h in range(NY * NZ)])]
    pallas_call x0 -> x1, Pallas kernels: none -> 0.75 us  [last_stage(): pl.pallas_call(last_kernel, in_specs=[vmem] * len(terms), out_specs=vmem,...]
  transfers between devices with their start and end apart: 22 -> 22, of which waited for: 11 -> 6; matrix products, arithmetic and copies ran while one was open for 1% -> 1% of each run, Pallas kernels for 6% -> 7%
where the time goes in v2:
time: 67.6 us; the launch traced here: 67.5 us
  starting transfers between devices  43.9 us (65%)
  waiting for transfers between devices  13.5 us (20%)
  Pallas kernels  9.7 us (14%)
    ppermute x16, starting transfers between devices, halve(): lax.ppermute(value, 'head', [(h, h ^ STEPS[step]) for h in range(NY * NZ)])  35.2 us
    ppermute x16, waiting for transfers between devices, halve(): lax.ppermute(value, 'head', [(h, h ^ STEPS[step]) for h in range(NY * NZ)])  11.8 us
    ppermute x6, starting transfers between devices, swap(): return lax.ppermute(value, 'ctx', [(i, i ^ mask) for i in range(4)])  8.62 us
    pallas_call x1, Pallas kernels, mix_stage(): pl.pallas_call(mix_kernel, in_specs=[vmem] * 16, out_specs=[vmem] * (2 *...  3.08 us
    pallas_call x1, Pallas kernels, fetch_stage(): pl.pallas_call(fetch_kernel, in_specs=[vmem] * 2 + [hbm] * 4, out_specs=[...  2.32 us
    pallas_call x1, Pallas kernels, local_stage(): pl.pallas_call(local_kernel, in_specs=[vmem] * 4 + [pl.BlockSpec(memory_s...  2.21 us
    ppermute x6, waiting for transfers between devices, swap(): return lax.ppermute(value, 'ctx', [(i, i ^ mask) for i in range(4)])  1.67 us
    pallas_call x1, Pallas kernels, pack_stage(): pl.pallas_call(pack_kernel, in_specs=[hbm] * 7, out_specs=[vmem] * 6, out...  1.35 us
  transfers between devices with their start and end apart: 22, of which 6 were waited for; matrix products, arithmetic and copies ran while one was open for 1% of the time, Pallas kernels for 7%

profile of v2, /device:TPU:2, one launch (start us, length us, event | category | flops | bytes accessed | tf_op | source)
XLA Modules:
  0.0 67.5 jit_solution(1051824112397579311)
XLA Ops:
  0.0 1.4 %pack_states.1 = (bf16[144,512]{1,0:T(8,128)(2,1)S(1)}, bf16[144,512]{1,0:T(8,128)(2,1)S(1)}, f32[128,512]{1,0:T(8,128)S(1)}, f32[16,512]{1,0:T(8,128)S(1)}, f32...) custom-call(bf16[128,512]{1,0:T(8,128)(2,1)} %conv_hbm.1, bf16[128,512]{1,0:T(8,128)(2,1)} %val_hbm.1, f32[16,512]{1,0:T(8,128)} %rate_hbm.1, ...), custom_call_target="tpu_custom_call" | custom-call | tf_op jit(solution)/shard_map/pack_states/pallas_call | solution.py:56
  1.4 2.3 %collective-permute-start = (bf16[144,512]{1,0:T(8,128)(2,1)S(1)}, bf16[144,512]{1,0:T(8,128)(2,1)S(1)}, u32[]{:S(2)}, u32[]{:S(2)}) collective-permute-start(bf16[144,512]{1,0:T(8,128)(2,1)S(1)} %get-tuple-element.26.a0), channel_id=1, source_target_pairs={{0,64},{64,0},{128,192},{192,128},{1,65},{65,1},{129,193},{193,129... | collective-permute-start | bytes 442376 | tf_op jit(solution)/shard_map/ppermute | solution.py:317
  4.1 1.6 %collective-permute-start.1 = (bf16[144,512]{1,0:T(8,128)(2,1)S(1)}, bf16[144,512]{1,0:T(8,128)(2,1)S(1)}, u32[]{:S(2)}, u32[]{:S(2)}) collective-permute-start(bf16[144,512]{1,0:T(8,128)(2,1)S(1)} %get-tuple-element.26.a0), channel_id=1, source_target_pairs={{0,192},{64,128},{128,64},{192,0},{1,193},{65,129},{129,65},{193,1... | collective-permute-start | bytes 442376 | tf_op jit(solution)/shard_map/ppermute | solution.py:317
  7.5 1.5 %collective-permute-start.2 = (bf16[144,512]{1,0:T(8,128)(2,1)S(1)}, bf16[144,512]{1,0:T(8,128)(2,1)S(1)}, u32[]{:S(2)}, u32[]{:S(2)}) collective-permute-start(bf16[144,512]{1,0:T(8,128)(2,1)S(1)} %collective-permute-done.a1), channel_id=1, source_target_pairs={{0,192},{64,128},{128,64},{192,0},{1,193},{65,129},{129,65},{193,1... | collective-permute-start | bytes 442376 | tf_op jit(solution)/shard_map/ppermute | solution.py:317
  10.2 1.5 %collective-permute-start.5 = (bf16[144,512]{1,0:T(8,128)(2,1)S(1)}, bf16[144,512]{1,0:T(8,128)(2,1)S(1)}, u32[]{:S(2)}, u32[]{:S(2)}) collective-permute-start(bf16[144,512]{1,0:T(8,128)(2,1)S(1)} %collective-permute-done.4.b3), channel_id=1, source_target_pairs={{0,64},{64,0},{128,192},{192,128},{1,65},{65,1},{129,193},{193,129... | collective-permute-start | bytes 442376 | tf_op jit(solution)/shard_map/ppermute | solution.py:317
  11.6 2.2 %local_conv.1 = (f32[128,512]{1,0:T(8,128)S(1)}, bf16[256,8192]{1,0:T(8,128)(2,1)S(1)}) custom-call(f32[128,512]{1,0:T(8,128)S(1)} %get-tuple-element.28.p_ref, f32[16,512]{1,0:T(8,128)S(1)} %get-tuple-element.29.rate_ref, f32[16,512]{1,0:T(8,128)S(1)} %get-tuple-element.30.res_ref, f32[1,512]{1,0:T(1,128)S(1)} %get-tuple-element.31.skip_ref, ...), custom_call_target="tpu_custom_call" | custom-call | tf_op jit(solution)/shard_map/local_conv/pallas_call | solution.py:142
  13.9 2.3 %fetch_weight.1 = (f32[4,128,128]{2,1,0:T(8,128)S(1)}, f32[2,8,16,512]{3,2,1,0:T(8,128)S(1)}, bf16[128,512]{1,0:T(8,128)(2,1)S(1)}, bf16[128,512]{1,0:T(8,128)(2,1)S(1)}, bf16[256,8192]{1,0:T(8,128)(2,1)S(1)}) custom-call(f32[16,512]{1,0:T(8,128)S(1)} %get-tuple-element.29.rate_ref, f32[16,512]{1,0:T(8,128)S(1)} %get-tuple-element.30.res_ref, s32[8]{0:T(128)} %slot_hbm.1, ...), custom_call_target="tpu_custom_call" | custom-call | tf_op jit(solution)/shard_map/fetch_weight/pallas_call | solution.py:191
  16.2 3.1 %mix_project.1 = (bf16[8,48,512]{2,1,0:T(8,128)(2,1)S(1)}, bf16[8,48,512]{2,1,0:T(8,128)(2,1)S(1)}, bf16[8,16,512]{2,1,0:T(8,128)(2,1)S(1)}, bf16[8,16,512]{2,1,...) custom-call(bf16[144,512]{1,0:T(8,128)(2,1)S(1)} %get-tuple-element., ...), custom_call_target="tpu_custom_call" | custom-call | tf_op jit(solution)/shard_map/mix_project/pallas_call | solution.py:283
  19.3 3.1 %collective-permute-start.14 = (bf16[8,16,512]{2,1,0:T(8,128)(2,1)S(1)}, bf16[8,16,512]{2,1,0:T(8,128)(2,1)S(1)}, u32[]{:S(2)}, u32[]{:S(2)}) collective-permute-start(bf16[8,16,512]{2,1,0:T(8,128)(2,1)S(1)} %get-tuple-element.44), channel_id=1, source_target_pairs={{0,4},{4,0},{8,12},{12,8},{16,20},{20,16},{24,28},{28,24},{32,36},... | collective-permute-start | bytes 393224 | tf_op jit(solution)/shard_map/ppermute | solution.py:321
  22.4 4.5 %collective-permute-start.18 = (bf16[8,16,512]{2,1,0:T(8,128)(2,1)S(1)}, bf16[8,16,512]{2,1,0:T(8,128)(2,1)S(1)}, u32[]{:S(2)}, u32[]{:S(2)}) collective-permute-start(bf16[8,16,512]{2,1,0:T(8,128)(2,1)S(1)} %get-tuple-element.46), channel_id=1, source_target_pairs={{0,12},{4,8},{8,4},{12,0},{16,28},{20,24},{24,20},{28,16},{32,44},... | collective-permute-start | bytes 393224 | tf_op jit(solution)/shard_map/ppermute | solution.py:321
  26.8 1.6 %collective-permute-start.6 = (bf16[8,48,512]{2,1,0:T(8,128)(2,1)S(1)}, bf16[8,48,512]{2,1,0:T(8,128)(2,1)S(1)}, u32[]{:S(2)}, u32[]{:S(2)}) collective-permute-start(bf16[8,48,512]{2,1,0:T(8,128)(2,1)S(1)} %get-tuple-element.40), channel_id=1, source_target_pairs={{0,16},{4,20},{8,24},{12,28},{16,0},{20,4},{24,8},{28,12},{32,48},... | collective-permute-start | bytes 1179656 | tf_op jit(solution)/shard_map/ppermute | solution.py:321
  28.4 2.2 %collective-permute-start.10 = (bf16[8,48,512]{2,1,0:T(8,128)(2,1)S(1)}, bf16[8,48,512]{2,1,0:T(8,128)(2,1)S(1)}, u32[]{:S(2)}, u32[]{:S(2)}) collective-permute-start(bf16[8,48,512]{2,1,0:T(8,128)(2,1)S(1)} %get-tuple-element.42), channel_id=1, source_target_pairs={{0,48},{4,52},{8,56},{12,60},{16,32},{20,36},{24,40},{28,44},{32,1... | collective-permute-start | bytes 1179656 | tf_op jit(solution)/shard_map/ppermute | solution.py:321
  30.6 1.6 %collective-permute-start.15 = (bf16[4,16,512]{2,1,0:T(8,128)(2,1)S(1)}, bf16[4,16,512]{2,1,0:T(8,128)(2,1)S(1)}, u32[]{:S(2)}, u32[]{:S(2)}) collective-permute-start(bf16[4,16,512]{2,1,0:T(8,128)(2,1)S(1)} %add_convert_fusion.5), channel_id=1, source_target_pairs={{0,12},{4,8},{8,4},{12,0},{16,28},{20,24},{24,20},{28,16},{32,44},... | collective-permute-start | bytes 196616 | tf_op jit(solution)/shard_map/ppermute | solution.py:321
  32.2 2.0 %collective-permute-start.19 = (bf16[4,16,512]{2,1,0:T(8,128)(2,1)S(1)}, bf16[4,16,512]{2,1,0:T(8,128)(2,1)S(1)}, u32[]{:S(2)}, u32[]{:S(2)}) collective-permute-start(bf16[4,16,512]{2,1,0:T(8,128)(2,1)S(1)} %add_convert_fusion.4), channel_id=1, source_target_pairs={{0,4},{4,0},{8,12},{12,8},{16,20},{20,16},{24,28},{28,24},{32,36},... | collective-permute-start | bytes 196616 | tf_op jit(solution)/shard_map/ppermute | solution.py:321
  34.2 2.9 %collective-permute-done.15.refs_12_ = bf16[4,16,512]{2,1,0:T(8,128)(2,1)S(1)} collective-permute-done((bf16[4,16,512]{2,1,0:T(8,128)(2,1)S(1)}, bf16[4,16,512]{2,1,0:T(8,128)(2,1)S(1)}, u32[]{:S(2)}, u32[]{:S(2)}) %collective-permute-start.15) | collective-permute-done | bytes 65568 | tf_op jit(solution)/shard_map/ppermute | solution.py:321
  38.0 2.6 %collective-permute-start.20 = (bf16[2,16,512]{2,1,0:T(8,128)(2,1)S(1)}, bf16[2,16,512]{2,1,0:T(8,128)(2,1)S(1)}, u32[]{:S(2)}, u32[]{:S(2)}) collective-permute-start(bf16[2,16,512]{2,1,0:T(8,128)(2,1)S(1)} %add_convert_fusion.8), channel_id=1, source_target_pairs={{0,48},{4,52},{8,56},{12,60},{16,32},{20,36},{24,40},{28,44},{32,1... | collective-permute-start | bytes 98312 | tf_op jit(solution)/shard_map/ppermute | solution.py:321
  41.2 1.3 %collective-permute-start.17 = (bf16[1,16,512]{2,1,0:T(8,128)(2,1)S(1)}, bf16[1,16,512]{2,1,0:T(8,128)(2,1)S(1)}, u32[]{:S(2)}, u32[]{:S(2)}) collective-permute-start(bf16[1,16,512]{2,1,0:T(8,128)(2,1)S(1)} %add_convert_fusion.11), channel_id=1, source_target_pairs={{0,48},{4,52},{8,56},{12,60},{16,32},{20,36},{24,40},{28,44},{32,1... | collective-permute-start | bytes 49160 | tf_op jit(solution)/shard_map/ppermute | solution.py:321
  42.6 2.3 %collective-permute-start.7 = (bf16[4,48,512]{2,1,0:T(8,128)(2,1)S(1)}, bf16[4,48,512]{2,1,0:T(8,128)(2,1)S(1)}, u32[]{:S(2)}, u32[]{:S(2)}) collective-permute-start(bf16[4,48,512]{2,1,0:T(8,128)(2,1)S(1)} %add_convert_fusion.1), channel_id=1, source_target_pairs={{0,48},{4,52},{8,56},{12,60},{16,32},{20,36},{24,40},{28,44},{32,1... | collective-permute-start | bytes 589832 | tf_op jit(solution)/shard_map/ppermute | solution.py:321
  45.0 4.5 %collective-permute-done.7.refs_2_ = bf16[4,48,512]{2,1,0:T(8,128)(2,1)S(1)} collective-permute-done((bf16[4,48,512]{2,1,0:T(8,128)(2,1)S(1)}, bf16[4,48,512]{2,1,0:T(8,128)(2,1)S(1)}, u32[]{:S(2)}, u32[]{:S(2)}) %collective-permute-start.7) | collective-permute-done | bytes 196640 | tf_op jit(solution)/shard_map/ppermute | solution.py:321
  49.6 2.2 %collective-permute-start.8 = (bf16[2,48,512]{2,1,0:T(8,128)(2,1)S(1)}, bf16[2,48,512]{2,1,0:T(8,128)(2,1)S(1)}, u32[]{:S(2)}, u32[]{:S(2)}) collective-permute-start(bf16[2,48,512]{2,1,0:T(8,128)(2,1)S(1)} %add_convert_fusion.3), channel_id=1, source_target_pairs={{0,4},{4,0},{8,12},{12,8},{16,20},{20,16},{24,28},{28,24},{32,36},... | collective-permute-start | bytes 294920 | tf_op jit(solution)/shard_map/ppermute | solution.py:321
  51.8 3.4 %collective-permute-start.12 = (bf16[2,48,512]{2,1,0:T(8,128)(2,1)S(1)}, bf16[2,48,512]{2,1,0:T(8,128)(2,1)S(1)}, u32[]{:S(2)}, u32[]{:S(2)}) collective-permute-start(bf16[2,48,512]{2,1,0:T(8,128)(2,1)S(1)} %add_convert_fusion.2), channel_id=1, source_target_pairs={{0,12},{4,8},{8,4},{12,0},{16,28},{20,24},{24,20},{28,16},{32,44},... | collective-permute-start | bytes 294920 | tf_op jit(solution)/shard_map/ppermute | solution.py:321
  55.3 4.2 %collective-permute-start.9 = (bf16[1,48,512]{2,1,0:T(8,128)(2,1)S(1)}, bf16[1,48,512]{2,1,0:T(8,128)(2,1)S(1)}, u32[]{:S(2)}, u32[]{:S(2)}) collective-permute-start(bf16[1,48,512]{2,1,0:T(8,128)(2,1)S(1)} %add_convert_fusion.7), channel_id=1, source_target_pairs={{0,12},{4,8},{8,4},{12,0},{16,28},{20,24},{24,20},{28,16},{32,44},... | collective-permute-start | bytes 147464 | tf_op jit(solution)/shard_map/ppermute | solution.py:321
  59.5 3.5 %collective-permute-start.13 = (bf16[1,48,512]{2,1,0:T(8,128)(2,1)S(1)}, bf16[1,48,512]{2,1,0:T(8,128)(2,1)S(1)}, u32[]{:S(2)}, u32[]{:S(2)}) collective-permute-start(bf16[1,48,512]{2,1,0:T(8,128)(2,1)S(1)} %add_convert_fusion.6), channel_id=1, source_target_pairs={{0,4},{4,0},{8,12},{12,8},{16,20},{20,16},{24,28},{28,24},{32,36},... | collective-permute-start | bytes 147464 | tf_op jit(solution)/shard_map/ppermute | solution.py:321
  63.1 3.7 %collective-permute-done.21.refs_19_ = bf16[1,16,512]{2,1,0:T(8,128)(2,1)S(1)} collective-permute-done((bf16[1,16,512]{2,1,0:T(8,128)(2,1)S(1)}, bf16[1,16,512]{2,1,0:T(8,128)(2,1)S(1)}, u32[]{:S(2)}, u32[]{:S(2)}) %collective-permute-start.21) | collective-permute-done | bytes 16416 | tf_op jit(solution)/shard_map/ppermute | solution.py:321
  (37 shorter events, 6.1 us)
Async XLA Ops:
  1.4 6.2 %collective-permute-start = (bf16[144,512]{1,0:T(8,128)(2,1)S(1)}, bf16[144,512]{1,0:T(8,128)(2,1)S(1)}, u32[]{:S(2)}, u32[]{:S(2)}) collective-permute-start(bf16[144,512]{1,0:T(8,128)(2,1)S(1)} %get-tuple-element.26.a0), channel_id=1, source_target_pairs={{0,64},{64,0},{128,192},{192,128},{1,65},{65,1},{129,193},{193,129... | collective-permute-start | bytes 442376 | tf_op jit(solution)/shard_map/ppermute | solution.py:317
  3.7 6.5 %collective-permute-start.4 = (bf16[144,512]{1,0:T(8,128)(2,1)S(1)}, bf16[144,512]{1,0:T(8,128)(2,1)S(1)}, u32[]{:S(2)}, u32[]{:S(2)}) collective-permute-start(bf16[144,512]{1,0:T(8,128)(2,1)S(1)} %get-tuple-element.27.b0), channel_id=1, source_target_pairs={{0,192},{64,128},{128,64},{192,0},{1,193},{65,129},{129,65},{193,1... | collective-permute-start | bytes 442376 | tf_op jit(solution)/shard_map/ppermute | solution.py:317
  4.1 12.0 %collective-permute-start.1 = (bf16[144,512]{1,0:T(8,128)(2,1)S(1)}, bf16[144,512]{1,0:T(8,128)(2,1)S(1)}, u32[]{:S(2)}, u32[]{:S(2)}) collective-permute-start(bf16[144,512]{1,0:T(8,128)(2,1)S(1)} %get-tuple-element.26.a0), channel_id=1, source_target_pairs={{0,192},{64,128},{128,64},{192,0},{1,193},{65,129},{129,65},{193,1... | collective-permute-start | bytes 442376 | tf_op jit(solution)/shard_map/ppermute | solution.py:317
  5.7 10.5 %collective-permute-start.3 = (bf16[144,512]{1,0:T(8,128)(2,1)S(1)}, bf16[144,512]{1,0:T(8,128)(2,1)S(1)}, u32[]{:S(2)}, u32[]{:S(2)}) collective-permute-start(bf16[144,512]{1,0:T(8,128)(2,1)S(1)} %get-tuple-element.27.b0), channel_id=1, source_target_pairs={{0,64},{64,0},{128,192},{192,128},{1,65},{65,1},{129,193},{193,129... | collective-permute-start | bytes 442376 | tf_op jit(solution)/shard_map/ppermute | solution.py:317
  7.5 8.7 %collective-permute-start.2 = (bf16[144,512]{1,0:T(8,128)(2,1)S(1)}, bf16[144,512]{1,0:T(8,128)(2,1)S(1)}, u32[]{:S(2)}, u32[]{:S(2)}) collective-permute-start(bf16[144,512]{1,0:T(8,128)(2,1)S(1)} %collective-permute-done.a1), channel_id=1, source_target_pairs={{0,192},{64,128},{128,64},{192,0},{1,193},{65,129},{129,65},{193,1... | collective-permute-start | bytes 442376 | tf_op jit(solution)/shard_map/ppermute | solution.py:317
  10.2 6.0 %collective-permute-start.5 = (bf16[144,512]{1,0:T(8,128)(2,1)S(1)}, bf16[144,512]{1,0:T(8,128)(2,1)S(1)}, u32[]{:S(2)}, u32[]{:S(2)}) collective-permute-start(bf16[144,512]{1,0:T(8,128)(2,1)S(1)} %collective-permute-done.4.b3), channel_id=1, source_target_pairs={{0,64},{64,0},{128,192},{192,128},{1,65},{65,1},{129,193},{193,129... | collective-permute-start | bytes 442376 | tf_op jit(solution)/shard_map/ppermute | solution.py:317
  19.3 11.3 %collective-permute-start.14 = (bf16[8,16,512]{2,1,0:T(8,128)(2,1)S(1)}, bf16[8,16,512]{2,1,0:T(8,128)(2,1)S(1)}, u32[]{:S(2)}, u32[]{:S(2)}) collective-permute-start(bf16[8,16,512]{2,1,0:T(8,128)(2,1)S(1)} %get-tuple-element.44), channel_id=1, source_target_pairs={{0,4},{4,0},{8,12},{12,8},{16,20},{20,16},{24,28},{28,24},{32,36},... | collective-permute-start | bytes 393224 | tf_op jit(solution)/shard_map/ppermute | solution.py:321
  22.4 9.9 %collective-permute-start.18 = (bf16[8,16,512]{2,1,0:T(8,128)(2,1)S(1)}, bf16[8,16,512]{2,1,0:T(8,128)(2,1)S(1)}, u32[]{:S(2)}, u32[]{:S(2)}) collective-permute-start(bf16[8,16,512]{2,1,0:T(8,128)(2,1)S(1)} %get-tuple-element.46), channel_id=1, source_target_pairs={{0,12},{4,8},{8,4},{12,0},{16,28},{20,24},{24,20},{28,16},{32,44},... | collective-permute-start | bytes 393224 | tf_op jit(solution)/shard_map/ppermute | solution.py:321
  26.8 15.7 %collective-permute-start.6 = (bf16[8,48,512]{2,1,0:T(8,128)(2,1)S(1)}, bf16[8,48,512]{2,1,0:T(8,128)(2,1)S(1)}, u32[]{:S(2)}, u32[]{:S(2)}) collective-permute-start(bf16[8,48,512]{2,1,0:T(8,128)(2,1)S(1)} %get-tuple-element.40), channel_id=1, source_target_pairs={{0,16},{4,20},{8,24},{12,28},{16,0},{20,4},{24,8},{28,12},{32,48},... | collective-permute-start | bytes 1179656 | tf_op jit(solution)/shard_map/ppermute | solution.py:321
  28.4 16.5 %collective-permute-start.10 = (bf16[8,48,512]{2,1,0:T(8,128)(2,1)S(1)}, bf16[8,48,512]{2,1,0:T(8,128)(2,1)S(1)}, u32[]{:S(2)}, u32[]{:S(2)}) collective-permute-start(bf16[8,48,512]{2,1,0:T(8,128)(2,1)S(1)} %get-tuple-element.42), channel_id=1, source_target_pairs={{0,48},{4,52},{8,56},{12,60},{16,32},{20,36},{24,40},{28,44},{32,1... | collective-permute-start | bytes 1179656 | tf_op jit(solution)/shard_map/ppermute | solution.py:321
  30.6 6.6 %collective-permute-start.15 = (bf16[4,16,512]{2,1,0:T(8,128)(2,1)S(1)}, bf16[4,16,512]{2,1,0:T(8,128)(2,1)S(1)}, u32[]{:S(2)}, u32[]{:S(2)}) collective-permute-start(bf16[4,16,512]{2,1,0:T(8,128)(2,1)S(1)} %add_convert_fusion.5), channel_id=1, source_target_pairs={{0,12},{4,8},{8,4},{12,0},{16,28},{20,24},{24,20},{28,16},{32,44},... | collective-permute-start | bytes 196616 | tf_op jit(solution)/shard_map/ppermute | solution.py:321
  32.2 5.7 %collective-permute-start.19 = (bf16[4,16,512]{2,1,0:T(8,128)(2,1)S(1)}, bf16[4,16,512]{2,1,0:T(8,128)(2,1)S(1)}, u32[]{:S(2)}, u32[]{:S(2)}) collective-permute-start(bf16[4,16,512]{2,1,0:T(8,128)(2,1)S(1)} %add_convert_fusion.4), channel_id=1, source_target_pairs={{0,4},{4,0},{8,12},{12,8},{16,20},{20,16},{24,28},{28,24},{32,36},... | collective-permute-start | bytes 196616 | tf_op jit(solution)/shard_map/ppermute | solution.py:321
  37.2 4.0 %collective-permute-start.16 = (bf16[2,16,512]{2,1,0:T(8,128)(2,1)S(1)}, bf16[2,16,512]{2,1,0:T(8,128)(2,1)S(1)}, u32[]{:S(2)}, u32[]{:S(2)}) collective-permute-start(bf16[2,16,512]{2,1,0:T(8,128)(2,1)S(1)} %add_convert_fusion.9), channel_id=1, source_target_pairs={{0,16},{4,20},{8,24},{12,28},{16,0},{20,4},{24,8},{28,12},{32,48},... | collective-permute-start | bytes 98312 | tf_op jit(solution)/shard_map/ppermute | solution.py:321
  38.0 24.9 %collective-permute-start.20 = (bf16[2,16,512]{2,1,0:T(8,128)(2,1)S(1)}, bf16[2,16,512]{2,1,0:T(8,128)(2,1)S(1)}, u32[]{:S(2)}, u32[]{:S(2)}) collective-permute-start(bf16[2,16,512]{2,1,0:T(8,128)(2,1)S(1)} %add_convert_fusion.8), channel_id=1, source_target_pairs={{0,48},{4,52},{8,56},{12,60},{16,32},{20,36},{24,40},{28,44},{32,1... | collective-permute-start | bytes 98312 | tf_op jit(solution)/shard_map/ppermute | solution.py:321
  41.2 21.8 %collective-permute-start.17 = (bf16[1,16,512]{2,1,0:T(8,128)(2,1)S(1)}, bf16[1,16,512]{2,1,0:T(8,128)(2,1)S(1)}, u32[]{:S(2)}, u32[]{:S(2)}) collective-permute-start(bf16[1,16,512]{2,1,0:T(8,128)(2,1)S(1)} %add_convert_fusion.11), channel_id=1, source_target_pairs={{0,48},{4,52},{8,56},{12,60},{16,32},{20,36},{24,40},{28,44},{32,1... | collective-permute-start | bytes 49160 | tf_op jit(solution)/shard_map/ppermute | solution.py:321
  42.6 7.0 %collective-permute-start.7 = (bf16[4,48,512]{2,1,0:T(8,128)(2,1)S(1)}, bf16[4,48,512]{2,1,0:T(8,128)(2,1)S(1)}, u32[]{:S(2)}, u32[]{:S(2)}) collective-permute-start(bf16[4,48,512]{2,1,0:T(8,128)(2,1)S(1)} %add_convert_fusion.1), channel_id=1, source_target_pairs={{0,48},{4,52},{8,56},{12,60},{16,32},{20,36},{24,40},{28,44},{32,1... | collective-permute-start | bytes 589832 | tf_op jit(solution)/shard_map/ppermute | solution.py:321
  44.9 6.8 %collective-permute-start.11 = (bf16[4,48,512]{2,1,0:T(8,128)(2,1)S(1)}, bf16[4,48,512]{2,1,0:T(8,128)(2,1)S(1)}, u32[]{:S(2)}, u32[]{:S(2)}) collective-permute-start(bf16[4,48,512]{2,1,0:T(8,128)(2,1)S(1)} %add_convert_fusion), channel_id=1, source_target_pairs={{0,16},{4,20},{8,24},{12,28},{16,0},{20,4},{24,8},{28,12},{32,48},... | collective-permute-start | bytes 589832 | tf_op jit(solution)/shard_map/ppermute | solution.py:321
  49.6 5.6 %collective-permute-start.8 = (bf16[2,48,512]{2,1,0:T(8,128)(2,1)S(1)}, bf16[2,48,512]{2,1,0:T(8,128)(2,1)S(1)}, u32[]{:S(2)}, u32[]{:S(2)}) collective-permute-start(bf16[2,48,512]{2,1,0:T(8,128)(2,1)S(1)} %add_convert_fusion.3), channel_id=1, source_target_pairs={{0,4},{4,0},{8,12},{12,8},{16,20},{20,16},{24,28},{28,24},{32,36},... | collective-permute-start | bytes 294920 | tf_op jit(solution)/shard_map/ppermute | solution.py:321
  51.8 7.6 %collective-permute-start.12 = (bf16[2,48,512]{2,1,0:T(8,128)(2,1)S(1)}, bf16[2,48,512]{2,1,0:T(8,128)(2,1)S(1)}, u32[]{:S(2)}, u32[]{:S(2)}) collective-permute-start(bf16[2,48,512]{2,1,0:T(8,128)(2,1)S(1)} %add_convert_fusion.2), channel_id=1, source_target_pairs={{0,12},{4,8},{8,4},{12,0},{16,28},{20,24},{24,20},{28,16},{32,44},... | collective-permute-start | bytes 294920 | tf_op jit(solution)/shard_map/ppermute | solution.py:321
  55.3 11.5 %collective-permute-start.9 = (bf16[1,48,512]{2,1,0:T(8,128)(2,1)S(1)}, bf16[1,48,512]{2,1,0:T(8,128)(2,1)S(1)}, u32[]{:S(2)}, u32[]{:S(2)}) collective-permute-start(bf16[1,48,512]{2,1,0:T(8,128)(2,1)S(1)} %add_convert_fusion.7), channel_id=1, source_target_pairs={{0,12},{4,8},{8,4},{12,0},{16,28},{20,24},{24,20},{28,16},{32,44},... | collective-permute-start | bytes 147464 | tf_op jit(solution)/shard_map/ppermute | solution.py:321
  59.5 7.3 %collective-permute-start.13 = (bf16[1,48,512]{2,1,0:T(8,128)(2,1)S(1)}, bf16[1,48,512]{2,1,0:T(8,128)(2,1)S(1)}, u32[]{:S(2)}, u32[]{:S(2)}) collective-permute-start(bf16[1,48,512]{2,1,0:T(8,128)(2,1)S(1)} %add_convert_fusion.6), channel_id=1, source_target_pairs={{0,4},{4,0},{8,12},{12,8},{16,20},{20,16},{24,28},{28,24},{32,36},... | collective-permute-start | bytes 147464 | tf_op jit(solution)/shard_map/ppermute | solution.py:321
  63.0 3.8 %collective-permute-start.21 = (bf16[1,16,512]{2,1,0:T(8,128)(2,1)S(1)}, bf16[1,16,512]{2,1,0:T(8,128)(2,1)S(1)}, u32[]{:S(2)}, u32[]{:S(2)}) collective-permute-start(bf16[1,16,512]{2,1,0:T(8,128)(2,1)S(1)} %add_convert_fusion.10), channel_id=1, source_target_pairs={{0,16},{4,20},{8,24},{12,28},{16,0},{20,4},{24,8},{28,12},{32,48},... | collective-permute-start | bytes 49160 | tf_op jit(solution)/shard_map/ppermute | solution.py:321
